TPU v7x, 32 devices: a whole 2x2x4 slice. The times are simulated.
32 devices in a mesh: row: 8 (over z, x), col: 4 (over y, core).
Axes of the slice: x: 2, y: 2, z: 4, core: 2. Of those that a mesh axis runs over, the one named last changes fastest.
Arguments:
- features: bfloat16 [64, 4096], P(None, ('col', 'row')), may hold values from -4 to 4
- targets: float32 [128, 4096], P(None, ('col', 'row')), may hold values from -6 to 6
Outputs:
- coefficients: float32 [128, 4096], P(None, ('col', 'row'))
- residual: float32 [128, 4096], P(None, ('col', 'row'))
- direction: float32 [128, 4096], P(None, ('col', 'row'))
All inputs are finite; a program needn't handle non-finite values.
Results may differ from a plain program's by a relative error of at most 0.0061.
Values may be sent and summed in bfloat16 or wider, within the bound.
No kernel may reach another device: no remote copies, remote signals or barrier semaphores. Data moves between devices by JAX's collectives and lax.ppermute only.
A program may use at most 64 MiB of HBM per device.

v0:
```python
import jax
import jax.numpy as jnp
from jax import lax
from jax.experimental import pallas as pl
from jax.experimental.pallas import tpu as pltpu
from jax.sharding import PartitionSpec as P

ridge_weight = 0.5
kernel_gain = 2.0
sharpness = 3.0
log2_e = 1.4426950408889634
longest = 4096
widest = 512
step_rows = 2048
product_vmem = 28 << 20
solve_vmem = 4 << 20

f32 = jnp.float32
bf16 = jnp.bfloat16


def product_kernel(columns, feat_rows, scale, finish):
    def body(*refs):
        if finish:
            *pieces, part_ref, z_ref, gram_ref, left, right, panel, sums = refs
        else:
            *pieces, part_ref, left, right, panel = refs
        per_piece, payload_rows, block = pieces[0].shape
        width = per_piece * block
        out_rows = payload_rows - feat_rows
        sub = min(width, widest)

        ones = jnp.ones((3, block), bf16)
        fill = jnp.zeros((10, block), bf16)
        used = [c[0] for c in columns]

        def prepare(j, b):
            at = j * width + b * block
            if not isinstance(b, int):
                at = pl.multiple_of(at, block)
            here = pl.ds(at, block)
            feat = pieces[j][b, :feat_rows, :]
            wide = feat.astype(f32)
            half = -0.5 * jnp.sum(wide * wide, axis=0, keepdims=True)
            high = half.astype(bf16)
            rest = half - high.astype(f32)
            mid = rest.astype(bf16)
            low = (rest - mid.astype(f32)).astype(bf16)
            norms = [high, mid, low]
            left[here, :] = jnp.concatenate([feat] + norms + [ones, fill], axis=0).T
            if j in used:
                right[:, here] = jnp.concatenate([feat, ones] + norms + [fill], axis=0)
            panel[:, here] = pieces[j][b, feat_rows:, :]

        for j in range(len(pieces)):
            if width <= widest:
                for b in range(per_piece):
                    prepare(j, b)
            else:
                lax.fori_loop(0, per_piece, lambda b, carry, j=j: (prepare(j, b), carry)[1], 0)

        def product(here, cols):
            inner = jnp.dot(left[here, :], right[:, cols], preferred_element_type=f32)
            entries = jnp.exp2(inner * (2.0 * scale * log2_e)).astype(bf16)
            return jnp.dot(panel[:, here], entries, preferred_element_type=f32)

        if finish:
            sums[...] = jnp.zeros(sums.shape, f32)

        def column(n, s):
            piece, first, last = columns[n]
            static = isinstance(s, int)
            at, to = piece * width + s * sub, n * width + s * sub
            if not static:
                at, to = pl.multiple_of(at, sub), pl.multiple_of(to, sub)
            cols = pl.ds(at, sub)
            if (last - first) * width <= longest:
                total = product(pl.ds(first * width, (last - first) * width), cols)
            else:
                steps = (last - first) * width // step_rows

                def add(t, carry):
                    start = pl.multiple_of(first * width + t * step_rows, step_rows)
                    return carry + product(pl.ds(start, step_rows), cols)

                total = lax.fori_loop(0, steps, add, jnp.zeros((out_rows, sub), f32))
            if not finish:
                part_ref[:, pl.ds(to, sub)] = total
                return
            if n * width < part_ref.shape[1]:
                total = total + part_ref[:, pl.ds(to, sub)]
            own_panel = panel[:, cols]
            z = total - own_panel.astype(f32)
            if n == 0:
                if static:
                    if s == 0:
                        z_ref[...] = z[:, :block]
                else:

                    @pl.when(s == 0)
                    def _():
                        z_ref[...] = z[:, :block]

            high = z.astype(bf16)
            low = (z - high.astype(f32)).astype(bf16)
            rhs = jnp.concatenate([own_panel, high], axis=0)
            lhs = jnp.concatenate([rhs, low], axis=0)
            sums[...] += lax.dot_general(lhs, rhs, (((1,), (1,)), ((), ())), preferred_element_type=f32)

        for n in range(len(columns)):
            if width == sub:
                column(n, 0)
            else:
                lax.fori_loop(0, width // sub, lambda s, carry, n=n: (column(n, s), carry)[1], 0)

        if finish:
            r = out_rows
            cross = sums[2 * r :, r:]
            gram_ref[0] = sums[:r, :r]
            gram_ref[1] = sums[r : 2 * r, :r] + sums[2 * r :, :r]
            gram_ref[2] = sums[r : 2 * r, r:] + cross + cross.T

    return body


def lanes(v, k):
    return jnp.broadcast_to(v[:, k : k + 1], v.shape)


def rows(v, j):
    return jnp.broadcast_to(v[j : j + 1, :], v.shape)


def negated_inverse(a, size):
    groups = size // 8
    lane = lax.broadcasted_iota(jnp.int32, (8, size), 1)
    sub = lax.broadcasted_iota(jnp.int32, (8, size), 0)

    def one_at(mask):
        return jnp.where(mask, 1.0, 0.0)

    one = one_at(lane >= 0)
    for q in range(groups):
        r = a[q]
        c = [lanes(r, 8 * q + m) * one for m in range(8)]
        for j in range(0, 8, 2):
            k = 8 * q + j
            p, b, d = rows(c[j], j), rows(c[j + 1], j), rows(c[j + 1], j + 1)
            scale = 1.0 / (p * d - b * b)
            c0 = c[j] - one_at(sub == j)
            c1 = c[j + 1] - one_at(sub == j + 1)
            u0 = (c0 * d - c1 * b) * scale
            u1 = (c1 * p - c0 * b) * scale
            for m in range(j + 2, 8):
                c[m] = c[m] - (u0 * rows(c[m], j) + u1 * rows(c[m], j + 1))
            fix = 2.0 * one_at(((lane == k) & (sub == j)) | ((lane == k + 1) & (sub == j + 1)))
            r = (r - fix) - (u0 * (rows(r, j) - one_at(lane == k)) + u1 * (rows(r, j + 1) - one_at(lane == k + 1)))
        w = r + one_at(lane - 8 * q == sub)
        w_rows = [rows(w, m) for m in range(8)]
        for i in range(q + 1, q + groups):
            x = a[i % groups]
            t = [lanes(x, 8 * q + m) * w_rows[m] for m in range(8)]
            a[i % groups] = x - (((t[0] + t[1]) + (t[2] + t[3])) + ((t[4] + t[5]) + (t[6] + t[7])))
        a[q] = r
    return a


def exact_dot(a, b):
    return jnp.dot(a, b, precision=lax.Precision.HIGHEST, preferred_element_type=f32)


def solve_kernel(mine, other, targets_ref, z_ref, coef_ref, res_ref, dir_ref):
    size = mine.shape[1]
    gram = mine[0] + other[0]
    mix_t = mine[1] + other[1]
    quad = mine[2] + other[2]
    diag = ridge_weight + kernel_gain
    mix = mix_t.T
    both = mix + mix_t
    half_gain = 0.5 * kernel_gain
    sym = diag * gram + half_gain * both
    outer = (diag * diag) * gram + (diag * kernel_gain) * both + (kernel_gain * kernel_gain) * quad
    curv = diag * gram + kernel_gain * mix
    eye = lax.broadcasted_iota(jnp.int32, (size, size), 0) == lax.broadcasted_iota(jnp.int32, (size, size), 1)
    on_diag = jnp.where(eye, sym, 0.0)
    by_col = lax.rsqrt(jnp.sum(on_diag, axis=0, keepdims=True))
    by_row = lax.rsqrt(jnp.sum(on_diag, axis=1, keepdims=True))
    unit = sym * by_row * by_col
    parts = negated_inverse([unit[8 * i : 8 * i + 8, :] for i in range(size // 8)], size)
    minus_inverse = jnp.concatenate(parts, axis=0) * by_row * by_col
    step_t = -exact_dot(gram, minus_inverse)
    correction_t = exact_dot(curv - exact_dot(step_t, outer), minus_inverse)
    targets = targets_ref[...]
    image = ridge_weight * targets + kernel_gain * (targets.astype(bf16).astype(f32) + z_ref[...])
    residual = targets - exact_dot(step_t, image)
    coef_ref[...] = exact_dot(step_t, targets)
    res_ref[...] = residual
    dir_ref[...] = residual + exact_dot(correction_t, targets)


def flips(size, bit):
    return [(i, i ^ bit) for i in range(size)]


def call(kernel, out_shape, scratch_shapes, operands, limit):
    vmem = pl.BlockSpec(memory_space=pltpu.VMEM)
    return pl.pallas_call(
        kernel,
        out_shape=out_shape,
        in_specs=[vmem] * len(operands),
        out_specs=jax.tree.map(lambda _: vmem, out_shape),
        scratch_shapes=scratch_shapes,
        compiler_params=pltpu.CompilerParams(vmem_limit_bytes=limit),
    )(*operands)


def local(row_size, col_size):
    def run(features, targets):
        return step(features, targets)

    def step(features, targets):
        feat_rows, block = features.shape
        out_rows = targets.shape[0]
        scale = sharpness / feat_rows

        def flip(axis, bit):
            size = row_size if axis == "row" else col_size
            return lambda x: lax.ppermute(x, axis, flips(size, bit))

        hops = [("row", 1 << s) for s in reversed(range(1, row_size.bit_length() - 1))]
        hops += [("col", 1 << s) for s in reversed(range(1, col_size.bit_length() - 2))]
        line = jnp.concatenate([features, targets.astype(bf16)], axis=0)[None]
        for axis, bit in hops:
            line = jnp.concatenate([line, flip(axis, bit)(line)], axis=0)
        over_x, over_y, partner = flip("row", 1), flip("col", col_size // 2), flip("col", 1)
        from_x, from_y = over_x(line), over_y(line)
        half = line.shape[0] // 2
        far_x = over_x(from_y[:half])
        far_y = over_y(from_x[half:])
        far = jnp.concatenate([far_x, far_y], axis=0)
        near = [line, from_x, from_y]
        other_near = [partner(x) for x in near]
        other_far = partner(far)

        width = line.shape[0] * block

        def scratch(count):
            return [
                pltpu.VMEM((count * width, feat_rows + 16), bf16),
                pltpu.VMEM((feat_rows + 16, count * width), bf16),
                pltpu.VMEM((out_rows, count * width), bf16),
            ]

        limit = product_vmem if width <= widest else None
        part = call(
            product_kernel([(0, 0, 6), (1, 0, 6), (2, 0, 6)], feat_rows, scale, False),
            jax.ShapeDtypeStruct((out_rows, 3 * width), f32),
            scratch(6),
            [*near, *other_near],
            limit,
        )
        z, grams = call(
            product_kernel([(0, 6, 8), (1, 6, 8), (2, 6, 8), (6, 0, 8)], feat_rows, scale, True),
            (
                jax.ShapeDtypeStruct((out_rows, block), f32),
                jax.ShapeDtypeStruct((3, out_rows, out_rows), f32),
            ),
            scratch(8) + [pltpu.VMEM((3 * out_rows, 2 * out_rows), f32)],
            [*near, *other_near, far, other_far, part],
            limit,
        )
        return call(
            solve_kernel,
            tuple(jax.ShapeDtypeStruct(targets.shape, f32) for _ in range(3)),
            [],
            [grams, partner(grams), targets, z],
            solve_vmem,
        )

    return run


def solution(mesh):
    spec = P(None, ("col", "row"))
    return jax.shard_map(
        local(mesh.shape["row"], mesh.shape["col"]),
        mesh=mesh,
        in_specs=(spec, spec),
        out_specs=(spec, spec, spec),
        check_vma=False,
    )
```

profile of v0, /device:TPU:0, one launch (start us, length us, event | category | flops | bytes accessed | tf_op | source)
XLA Modules:
  0.0 42.0 jit_solution(6621796339690736680)
XLA Ops:
  0.6 0.0 copy-start.1
  0.6 0.9 %convert_element_type.3 = bf16[128,128]{1,0:T(8,128)(2,1)S(1)} convert(f32[128,128]{1,0:T(8,128)} %targets_ref.1) | non-fusion elementwise | flops 16384 | bytes 98304 | tf_op jit(solution)/shard_map/convert_element_type | solution.py:232
  1.5 0.0 copy-done.1
  1.5 4.1 %collective-permute-start = (bf16[1,192,128]{2,1,0:T(8,128)(2,1)S(1)}, bf16[1,192,128]{2,1,0:T(8,128)(2,1)S(1)}, u32[]{:S(2)}, u32[]{:S(2)}) collective-permute-start(bf16[1,192,128]{2,1,0:T(8,128)(2,1)S(1)} %maximum_bitcast_fusion), channel_id=1, source_target_pairs={{0,16},{4,20},{8,24},{12,28},{16,0},{20,4},{24,8},{28,12},{1,17},{... | collective-permute-start | bytes 147464 | tf_op jit(solution)/shard_map/ppermute | solution.py:228
  5.6 2.6 %collective-permute-done = bf16[1,192,128]{2,1,0:T(8,128)(2,1)S(1)} collective-permute-done((bf16[1,192,128]{2,1,0:T(8,128)(2,1)S(1)}, bf16[1,192,128]{2,1,0:T(8,128)(2,1)S(1)}, u32[]{:S(2)}, u32[]{:S(2)}) %collective-permute-start) | collective-permute-done | bytes 49184 | tf_op jit(solution)/shard_map/ppermute | solution.py:228
  8.2 1.4 %collective-permute-start.1 = (bf16[2,192,128]{2,1,0:T(8,128)(2,1)S(1)}, bf16[2,192,128]{2,1,0:T(8,128)(2,1)S(1)}, u32[]{:S(2)}, u32[]{:S(2)}) collective-permute-start(bf16[2,192,128]{2,1,0:T(8,128)(2,1)S(1)} %pad_maximum_fusion.1), channel_id=1, source_target_pairs={{0,8},{4,12},{8,0},{12,4},{16,24},{20,28},{24,16},{28,20},{1,9},{5... | collective-permute-start | bytes 294920 | tf_op jit(solution)/shard_map/ppermute | solution.py:228
  9.7 3.2 %collective-permute-done.1 = bf16[2,192,128]{2,1,0:T(8,128)(2,1)S(1)} collective-permute-done((bf16[2,192,128]{2,1,0:T(8,128)(2,1)S(1)}, bf16[2,192,128]{2,1,0:T(8,128)(2,1)S(1)}, u32[]{:S(2)}, u32[]{:S(2)}) %collective-permute-start.1) | collective-permute-done | bytes 98336 | tf_op jit(solution)/shard_map/ppermute | solution.py:228
  12.9 1.8 %collective-permute-start.3 = (bf16[4,192,128]{2,1,0:T(8,128)(2,1)S(1)}, bf16[4,192,128]{2,1,0:T(8,128)(2,1)S(1)}, u32[]{:S(2)}, u32[]{:S(2)}) collective-permute-start(bf16[4,192,128]{2,1,0:T(8,128)(2,1)S(1)} %pad_maximum_fusion.refs_0_), channel_id=1, source_target_pairs={{0,2},{1,3},{2,0},{3,1},{4,6},{5,7},{6,4},{7,5},{8,10},{9,11},{10,... | collective-permute-start | bytes 589832 | tf_op jit(solution)/shard_map/ppermute | solution.py:228
  14.7 1.5 %collective-permute-start.2 = (bf16[4,192,128]{2,1,0:T(8,128)(2,1)S(1)}, bf16[4,192,128]{2,1,0:T(8,128)(2,1)S(1)}, u32[]{:S(2)}, u32[]{:S(2)}) collective-permute-start(bf16[4,192,128]{2,1,0:T(8,128)(2,1)S(1)} %pad_maximum_fusion.refs_0_), channel_id=1, source_target_pairs={{0,4},{4,0},{8,12},{12,8},{16,20},{20,16},{24,28},{28,24},{1,5},{5... | collective-permute-start | bytes 589832 | tf_op jit(solution)/shard_map/ppermute | solution.py:228
  16.2 2.5 %collective-permute-done.3.refs_2_ = bf16[4,192,128]{2,1,0:T(8,128)(2,1)S(1)} collective-permute-done((bf16[4,192,128]{2,1,0:T(8,128)(2,1)S(1)}, bf16[4,192,128]{2,1,0:T(8,128)(2,1)S(1)}, u32[]{:S(2)}, u32[]{:S(2)}) %collective-permute-start.3) | collective-permute-done | bytes 196640 | tf_op jit(solution)/shard_map/ppermute | solution.py:228
  18.7 1.8 %collective-permute-start.7 = (bf16[2,192,128]{2,1,0:T(8,128)(2,1)S(1)}, bf16[2,192,128]{2,1,0:T(8,128)(2,1)S(1)}, u32[]{:S(2)}, u32[]{:S(2)}) collective-permute-start(bf16[2,192,128]{2,1,0:T(8,128)(2,1)S(1)} %slice.8), channel_id=1, source_target_pairs={{0,4},{4,0},{8,12},{12,8},{16,20},{20,16},{24,28},{28,24},{1,5},{5... | collective-permute-start | bytes 294920 | tf_op jit(solution)/shard_map/ppermute | solution.py:228
  20.5 0.0 collective-permute-start.4
  20.5 0.2 collective-permute-done.2.refs_1_
  20.7 1.4 %collective-permute-start.8 = (bf16[2,192,128]{2,1,0:T(8,128)(2,1)S(1)}, bf16[2,192,128]{2,1,0:T(8,128)(2,1)S(1)}, u32[]{:S(2)}, u32[]{:S(2)}) collective-permute-start(bf16[2,192,128]{2,1,0:T(8,128)(2,1)S(1)} %slice.9), channel_id=1, source_target_pairs={{0,2},{1,3},{2,0},{3,1},{4,6},{5,7},{6,4},{7,5},{8,10},{9,11},{10,... | collective-permute-start | bytes 294920 | tf_op jit(solution)/shard_map/ppermute | solution.py:228
  22.1 0.2 collective-permute-start.6
  22.3 0.3 collective-permute-start.5
  22.6 0.8 %collective-permute-done.7 = bf16[2,192,128]{2,1,0:T(8,128)(2,1)S(1)} collective-permute-done((bf16[2,192,128]{2,1,0:T(8,128)(2,1)S(1)}, bf16[2,192,128]{2,1,0:T(8,128)(2,1)S(1)}, u32[]{:S(2)}, u32[]{:S(2)}) %collective-permute-start.7) | collective-permute-done | bytes 98336 | tf_op jit(solution)/shard_map/ppermute | solution.py:228
  23.4 2.4 %collective-permute-done.8 = bf16[2,192,128]{2,1,0:T(8,128)(2,1)S(1)} collective-permute-done((bf16[2,192,128]{2,1,0:T(8,128)(2,1)S(1)}, bf16[2,192,128]{2,1,0:T(8,128)(2,1)S(1)}, u32[]{:S(2)}, u32[]{:S(2)}) %collective-permute-start.8) | collective-permute-done | bytes 98336 | tf_op jit(solution)/shard_map/ppermute | solution.py:228
  25.8 0.1 collective-permute-start.9
  25.8 0.0 collective-permute-done.4.refs_3_
  25.9 0.0 collective-permute-done.6.refs_5_
  25.9 0.0 collective-permute-done.5.refs_4_
  25.9 4.3 %shard_map.49.refs_8_ = f32[128,1536]{1,0:T(8,128)S(1)} custom-call(bf16[4,192,128]{2,1,0:T(8,128)(2,1)S(1)} %pad_maximum_fusion.refs_0_, bf16[4,192,128]{2,1,0:T(8,128)(2,1)S(1)} %collective-permute-done.2.refs_1_, bf16[4,192,128]{2,1,0:T(8,128)(2,1)S(1)} %collective-permute-done.3.refs_2_, bf16[4,192,128]{2,1,0:T(8,128)(2,1)S(1)} %collective-permute-done.4.refs_3_, ...), custom_call_target="tpu_custom_call" | custom-call | tf_op jit(solution)/shard_map/pallas_call | solution.py:207
  30.2 0.0 copy-start
  30.2 0.0 collective-permute-done.9.refs_7_
  30.2 4.6 %shard_map.50 = (f32[128,128]{1,0:T(8,128)S(1)}, f32[3,128,128]{2,1,0:T(8,128)S(1)}) custom-call(bf16[4,192,128]{2,1,0:T(8,128)(2,1)S(1)} %pad_maximum_fusion.refs_0_, bf16[4,192,128]{2,1,0:T(8,128)(2,1)S(1)} %collective-permute-done.2.refs_1_, bf16[4,192,128]{2,1,0:T(8,128)(2,1)S(1)} %collective-permute-done.3.refs_2_, ...), custom_call_target="tpu_custom_call" | custom-call | tf_op jit(solution)/shard_map/pallas_call | solution.py:207
  34.8 0.5 %collective-permute-start.10 = (f32[3,128,128]{2,1,0:T(8,128)S(1)}, f32[3,128,128]{2,1,0:T(8,128)S(1)}, u32[]{:S(2)}, u32[]{:S(2)}) collective-permute-start(f32[3,128,128]{2,1,0:T(8,128)S(1)} %get-tuple-element.5.mine), channel_id=1, source_target_pairs={{0,1},{1,0},{2,3},{3,2},{4,5},{5,4},{6,7},{7,6},{8,9},{9,8},{10,11... | collective-permute-start | bytes 589832 | tf_op jit(solution)/shard_map/ppermute | solution.py:228
  35.4 1.1 %collective-permute-done.10.other = f32[3,128,128]{2,1,0:T(8,128)S(1)} collective-permute-done((f32[3,128,128]{2,1,0:T(8,128)S(1)}, f32[3,128,128]{2,1,0:T(8,128)S(1)}, u32[]{:S(2)}, u32[]{:S(2)}) %collective-permute-start.10) | collective-permute-done | bytes 196640 | tf_op jit(solution)/shard_map/ppermute | solution.py:228
  36.4 0.0 copy-done
  36.4 5.6 %shard_map.51 = (f32[128,128]{1,0:T(8,128)}, f32[128,128]{1,0:T(8,128)}, f32[128,128]{1,0:T(8,128)}) custom-call(f32[3,128,128]{2,1,0:T(8,128)S(1)} %get-tuple-element.5.mine, f32[3,128,128]{2,1,0:T(8,128)S(1)} %collective-permute-done.10.other, f32[128,128]{1,0:T(8,128)S(1)} %copy-done, f32[128,128]{1,0:T(8,128)S(1)} %get-tuple-element.6.z_ref), custom_call_target="tpu_custom_call" | custom-call | tf_op jit(solution)/shard_map/pallas_call | solution.py:207
  (7 shorter events, 0.1 us)
Async XLA Ops:
  0.6 0.9 %copy-start.1 = (bf16[64,128]{1,0:T(8,128)(2,1)S(1)}, bf16[64,128]{1,0:T(8,128)(2,1)}, u32[]{:S(2)}) copy-start(bf16[64,128]{1,0:T(8,128)(2,1)} %param.2) | copy-start | bytes 49156
  1.5 6.7 %collective-permute-start = (bf16[1,192,128]{2,1,0:T(8,128)(2,1)S(1)}, bf16[1,192,128]{2,1,0:T(8,128)(2,1)S(1)}, u32[]{:S(2)}, u32[]{:S(2)}) collective-permute-start(bf16[1,192,128]{2,1,0:T(8,128)(2,1)S(1)} %maximum_bitcast_fusion), channel_id=1, source_target_pairs={{0,16},{4,20},{8,24},{12,28},{16,0},{20,4},{24,8},{28,12},{1,17},{... | collective-permute-start | bytes 147464 | tf_op jit(solution)/shard_map/ppermute | solution.py:228
  8.2 4.7 %collective-permute-start.1 = (bf16[2,192,128]{2,1,0:T(8,128)(2,1)S(1)}, bf16[2,192,128]{2,1,0:T(8,128)(2,1)S(1)}, u32[]{:S(2)}, u32[]{:S(2)}) collective-permute-start(bf16[2,192,128]{2,1,0:T(8,128)(2,1)S(1)} %pad_maximum_fusion.1), channel_id=1, source_target_pairs={{0,8},{4,12},{8,0},{12,4},{16,24},{20,28},{24,16},{28,20},{1,9},{5... | collective-permute-start | bytes 294920 | tf_op jit(solution)/shard_map/ppermute | solution.py:228
  12.9 5.7 %collective-permute-start.3 = (bf16[4,192,128]{2,1,0:T(8,128)(2,1)S(1)}, bf16[4,192,128]{2,1,0:T(8,128)(2,1)S(1)}, u32[]{:S(2)}, u32[]{:S(2)}) collective-permute-start(bf16[4,192,128]{2,1,0:T(8,128)(2,1)S(1)} %pad_maximum_fusion.refs_0_), channel_id=1, source_target_pairs={{0,2},{1,3},{2,0},{3,1},{4,6},{5,7},{6,4},{7,5},{8,10},{9,11},{10,... | collective-permute-start | bytes 589832 | tf_op jit(solution)/shard_map/ppermute | solution.py:228
  14.7 5.9 %collective-permute-start.2 = (bf16[4,192,128]{2,1,0:T(8,128)(2,1)S(1)}, bf16[4,192,128]{2,1,0:T(8,128)(2,1)S(1)}, u32[]{:S(2)}, u32[]{:S(2)}) collective-permute-start(bf16[4,192,128]{2,1,0:T(8,128)(2,1)S(1)} %pad_maximum_fusion.refs_0_), channel_id=1, source_target_pairs={{0,4},{4,0},{8,12},{12,8},{16,20},{20,16},{24,28},{28,24},{1,5},{5... | collective-permute-start | bytes 589832 | tf_op jit(solution)/shard_map/ppermute | solution.py:228
  18.7 4.7 %collective-permute-start.7 = (bf16[2,192,128]{2,1,0:T(8,128)(2,1)S(1)}, bf16[2,192,128]{2,1,0:T(8,128)(2,1)S(1)}, u32[]{:S(2)}, u32[]{:S(2)}) collective-permute-start(bf16[2,192,128]{2,1,0:T(8,128)(2,1)S(1)} %slice.8), channel_id=1, source_target_pairs={{0,4},{4,0},{8,12},{12,8},{16,20},{20,16},{24,28},{28,24},{1,5},{5... | collective-permute-start | bytes 294920 | tf_op jit(solution)/shard_map/ppermute | solution.py:228
  20.5 5.4 %collective-permute-start.4 = (bf16[4,192,128]{2,1,0:T(8,128)(2,1)S(1)}, bf16[4,192,128]{2,1,0:T(8,128)(2,1)S(1)}, u32[]{:S(2)}, u32[]{:S(2)}) collective-permute-start(bf16[4,192,128]{2,1,0:T(8,128)(2,1)S(1)} %pad_maximum_fusion.refs_0_), channel_id=1, source_target_pairs={{0,1},{1,0},{2,3},{3,2},{4,5},{5,4},{6,7},{7,6},{8,9},{9,8},{10,11... | collective-permute-start | bytes 589832 | tf_op jit(solution)/shard_map/ppermute | solution.py:228
  20.7 5.1 %collective-permute-start.8 = (bf16[2,192,128]{2,1,0:T(8,128)(2,1)S(1)}, bf16[2,192,128]{2,1,0:T(8,128)(2,1)S(1)}, u32[]{:S(2)}, u32[]{:S(2)}) collective-permute-start(bf16[2,192,128]{2,1,0:T(8,128)(2,1)S(1)} %slice.9), channel_id=1, source_target_pairs={{0,2},{1,3},{2,0},{3,1},{4,6},{5,7},{6,4},{7,5},{8,10},{9,11},{10,... | collective-permute-start | bytes 294920 | tf_op jit(solution)/shard_map/ppermute | solution.py:228
  22.1 3.8 %collective-permute-start.6 = (bf16[4,192,128]{2,1,0:T(8,128)(2,1)S(1)}, bf16[4,192,128]{2,1,0:T(8,128)(2,1)S(1)}, u32[]{:S(2)}, u32[]{:S(2)}) collective-permute-start(bf16[4,192,128]{2,1,0:T(8,128)(2,1)S(1)} %collective-permute-done.3.refs_2_), channel_id=1, source_target_pairs={{0,1},{1,0},{2,3},{3,2},{4,5},{5,4},{6,7},{7,6},{8,9},{9,8},{10,11... | collective-permute-start | bytes 589832 | tf_op jit(solution)/shard_map/ppermute | solution.py:228
  22.3 3.6 %collective-permute-start.5 = (bf16[4,192,128]{2,1,0:T(8,128)(2,1)S(1)}, bf16[4,192,128]{2,1,0:T(8,128)(2,1)S(1)}, u32[]{:S(2)}, u32[]{:S(2)}) collective-permute-start(bf16[4,192,128]{2,1,0:T(8,128)(2,1)S(1)} %collective-permute-done.2.refs_1_), channel_id=1, source_target_pairs={{0,1},{1,0},{2,3},{3,2},{4,5},{5,4},{6,7},{7,6},{8,9},{9,8},{10,11... | collective-permute-start | bytes 589832 | tf_op jit(solution)/shard_map/ppermute | solution.py:228
  25.8 4.4 %collective-permute-start.9 = (bf16[4,192,128]{2,1,0:T(8,128)(2,1)S(1)}, bf16[4,192,128]{2,1,0:T(8,128)(2,1)S(1)}, u32[]{:S(2)}, u32[]{:S(2)}) collective-permute-start(bf16[4,192,128]{2,1,0:T(8,128)(2,1)S(1)} %constant_dynamic-update-slice_fusion.refs_6_), channel_id=1, source_target_pairs={{0,1},{1,0},{2,3},{3,2},{4,5},{5,4},{6,7},{7,6},{8,9},{9,8},{10,11... | collective-permute-start | bytes 589832 | tf_op jit(solution)/shard_map/ppermute | solution.py:228
  30.2 6.2 %copy-start = (f32[128,128]{1,0:T(8,128)S(1)}, f32[128,128]{1,0:T(8,128)}, u32[]{:S(2)}) copy-start(f32[128,128]{1,0:T(8,128)} %targets_ref.1) | copy-start | bytes 196612
  34.8 1.6 %collective-permute-start.10 = (f32[3,128,128]{2,1,0:T(8,128)S(1)}, f32[3,128,128]{2,1,0:T(8,128)S(1)}, u32[]{:S(2)}, u32[]{:S(2)}) collective-permute-start(f32[3,128,128]{2,1,0:T(8,128)S(1)} %get-tuple-element.5.mine), channel_id=1, source_target_pairs={{0,1},{1,0},{2,3},{3,2},{4,5},{5,4},{6,7},{7,6},{8,9},{9,8},{10,11... | collective-permute-start | bytes 589832 | tf_op jit(solution)/shard_map/ppermute | solution.py:228
where the time goes:
time: 42.2 us; the launch traced here: 42 us
  Pallas kernels  14.5 us (34%)
  starting transfers between devices  13.1 us (31%)
  waiting for transfers between devices  12.7 us (30%)
  other arithmetic  0.89 us (2%)
  between operations  0.73 us (2%)
    pallas_call x3, Pallas kernels, call(): pl.pallas_call(kernel, out_shape=out_shape, in_specs=[vmem] * len(operand...  14.5 us
    ppermute x11, starting transfers between devices, flip(): return lambda x: lax.ppermute(x, axis, flips(size, bit))  13.1 us
    ppermute x11, waiting for transfers between devices, flip(): return lambda x: lax.ppermute(x, axis, flips(size, bit))  12.7 us
    convert_element_type x1, other arithmetic, step(): line = jnp.concatenate([features, targets.astype(bf16)], axis=0)[None]  0.85 us
  transfers between devices with their start and end apart: 11, of which 7 were waited for; matrix products, arithmetic and copies ran while one was open for 0% of the time, Pallas kernels for 10%

commit v1 on v0

v1 whole, which is shorter than its diff:
```python
import jax
import jax.numpy as jnp
from jax import lax
from jax.experimental import pallas as pl
from jax.experimental.pallas import tpu as pltpu
from jax.sharding import PartitionSpec as P

ridge_weight = 0.5
kernel_gain = 2.0
sharpness = 3.0
log2_e = 1.4426950408889634
longest = 4096
widest = 1024
step_rows = 2048
step_cols = 512
product_vmem = 28 << 20
solve_vmem = 4 << 20

f32 = jnp.float32
bf16 = jnp.bfloat16


def prepare(own, other, left, right, panel, feat_rows):
    count, _, block = (other if own is None else own).shape
    ones = jnp.ones((3, block), bf16)
    fill = jnp.zeros((10, block), bf16)

    def one(piece, at, b, is_own):
        here = pl.ds(at, block)
        feat = piece[b, :feat_rows, :]
        wide = feat.astype(f32)
        half = -0.5 * jnp.sum(wide * wide, axis=0, keepdims=True)
        high = half.astype(bf16)
        rest = half - high.astype(f32)
        mid = rest.astype(bf16)
        low = (rest - mid.astype(f32)).astype(bf16)
        norms = [high, mid, low]
        left[here, :] = jnp.concatenate([feat] + norms + [ones, fill], axis=0).T
        if is_own:
            right[:, here] = jnp.concatenate([feat, ones] + norms + [fill], axis=0)
        panel[:, here] = piece[b, feat_rows:, :]

    for piece, first in ((own, 0), (other, count)):
        if piece is None:
            continue
        if count <= 8:
            for b in range(count):
                one(piece, (first + b) * block, b, piece is own)
        else:

            def looped(b, carry, piece=piece, first=first):
                one(piece, pl.multiple_of((first + b) * block, block), b, piece is own)
                return carry

            lax.fori_loop(0, count, looped, 0)


def product(stage, right, cols, scale):
    left, panel = stage
    rows_of = left.shape[0]

    def part(here):
        inner = jnp.dot(left[here, :], right[:, cols], preferred_element_type=f32)
        entries = jnp.exp2(inner * (2.0 * scale * log2_e)).astype(bf16)
        return jnp.dot(panel[:, here], entries, preferred_element_type=f32)

    if rows_of <= longest:
        return part(slice(None))

    def add(t, carry):
        return carry + part(pl.ds(pl.multiple_of(t * step_rows, step_rows), step_rows))

    return lax.fori_loop(0, rows_of // step_rows, add, jnp.zeros((panel.shape[0], cols.size), f32))


def over_columns(count, work):
    if count <= widest:
        work(pl.ds(0, count), True)
    else:

        def looped(s, carry):
            work(pl.ds(pl.multiple_of(s * step_cols, step_cols), step_cols), s == 0)
            return carry

        lax.fori_loop(0, count // step_cols, looped, 0)


def first_kernel(feat_rows, scale):
    def body(own, other, left, right, panel, y0):
        prepare(own, other, left, right, panel, feat_rows)

        def work(cols, _):
            y0[:, cols] = product((left, panel), right, cols, scale)

        over_columns(right.shape[1], work)

    return body


def second_kernel(feat_rows, scale):
    def body(own, other, left0, right0, panel0, y0_in, left, right, panel, y0, y1):
        prepare(own, other, left, right, panel, feat_rows)
        now, before = (left, panel), (left0, panel0)

        def work1(cols, _):
            y1[:, cols] = product(before, right, cols, scale) + product(now, right, cols, scale)

        def work0(cols, _):
            y0[:, cols] = y0_in[:, cols] + product(now, right0, cols, scale)

        over_columns(right.shape[1], work1)
        over_columns(right0.shape[1], work0)

    return body


def cover_kernel(feat_rows, scale):
    def body(own, left0, panel0, left1, panel1, left, right, panel, y2):
        prepare(own, None, left, right, panel, feat_rows)

        def work(cols, _):
            y2[:, cols] = product((left0, panel0), right, cols, scale) + product((left1, panel1), right, cols, scale)

        over_columns(right.shape[1], work)

    return body


def third_kernel(feat_rows, scale):
    def body(other, *refs):
        left_own, right, panel_own, right0, panel0, right1, panel1, y0, y1, y2, z_ref, gram_ref, left, panel, sums = refs
        mine = right.shape[1]
        left[:mine, :] = left_own[...]
        panel[:, :mine] = panel_own[...]
        prepare(None, other, left, right, panel, feat_rows)
        sums[...] = jnp.zeros(sums.shape, f32)
        block = z_ref.shape[1]

        def add_columns(right_of, panel_of, y, holds_own):
            def work(cols, is_first):
                total = product((left, panel), right_of, cols, scale) + y[:, cols]
                own_panel = panel_of[:, cols]
                z = total - own_panel.astype(f32)
                if holds_own:

                    def put():
                        z_ref[...] = z[:, :block]

                    put() if is_first is True else pl.when(is_first)(put)
                high = z.astype(bf16)
                low = (z - high.astype(f32)).astype(bf16)
                rhs = jnp.concatenate([own_panel, high], axis=0)
                lhs = jnp.concatenate([rhs, low], axis=0)
                sums[...] += lax.dot_general(lhs, rhs, (((1,), (1,)), ((), ())), preferred_element_type=f32)

            over_columns(right_of.shape[1], work)

        add_columns(right0, panel0, y0, True)
        add_columns(right1, panel1, y1, False)
        add_columns(right, panel, y2, False)
        r = panel.shape[0]
        cross = sums[2 * r :, r:]
        gram_ref[0] = sums[:r, :r]
        gram_ref[1] = sums[r : 2 * r, :r] + sums[2 * r :, :r]
        gram_ref[2] = sums[r : 2 * r, r:] + cross + cross.T

    return body


def lanes(v, k):
    return jnp.broadcast_to(v[:, k : k + 1], v.shape)


def rows(v, j):
    return jnp.broadcast_to(v[j : j + 1, :], v.shape)


def negated_inverse(a, size):
    groups = size // 8
    lane = lax.broadcasted_iota(jnp.int32, (8, size), 1)
    sub = lax.broadcasted_iota(jnp.int32, (8, size), 0)

    def one_at(mask):
        return jnp.where(mask, 1.0, 0.0)

    one = one_at(lane >= 0)
    for q in range(groups):
        r = a[q]
        c = [lanes(r, 8 * q + m) * one for m in range(8)]
        for j in range(0, 8, 2):
            k = 8 * q + j
            p, b, d = rows(c[j], j), rows(c[j + 1], j), rows(c[j + 1], j + 1)
            scale = 1.0 / (p * d - b * b)
            c0 = c[j] - one_at(sub == j)
            c1 = c[j + 1] - one_at(sub == j + 1)
            u0 = (c0 * d - c1 * b) * scale
            u1 = (c1 * p - c0 * b) * scale
            for m in range(j + 2, 8):
                c[m] = c[m] - (u0 * rows(c[m], j) + u1 * rows(c[m], j + 1))
            fix = 2.0 * one_at(((lane == k) & (sub == j)) | ((lane == k + 1) & (sub == j + 1)))
            r = (r - fix) - (u0 * (rows(r, j) - one_at(lane == k)) + u1 * (rows(r, j + 1) - one_at(lane == k + 1)))
        w = r + one_at(lane - 8 * q == sub)
        w_rows = [rows(w, m) for m in range(8)]
        base = groups // 2 if q < groups // 2 else 0
        update = lax.dot_general(
            a[q][:, 8 * base : 8 * base + size // 2],
            w,
            (((0,), (0,)), ((), ())),
            precision=lax.Precision.HIGHEST,
            preferred_element_type=f32,
        )
        for i in [i % groups for i in range(q + 1, q + groups)]:
            x = a[i]
            at = 8 * (i - base)
            if 0 <= at < size // 2 and i != q + 1:
                a[i] = x - update[at : at + 8, :]
            else:
                t = [lanes(x, 8 * q + m) * w_rows[m] for m in range(8)]
                a[i] = x - (((t[0] + t[1]) + (t[2] + t[3])) + ((t[4] + t[5]) + (t[6] + t[7])))
        a[q] = r
    return a


def exact_dot(a, b):
    return jnp.dot(a, b, precision=lax.Precision.HIGHEST, preferred_element_type=f32)


def solve_kernel(mine, other, targets_ref, z_ref, coef_ref, res_ref, dir_ref):
    size = mine.shape[1]
    gram = mine[0] + other[0]
    mix_t = mine[1] + other[1]
    quad = mine[2] + other[2]
    diag = ridge_weight + kernel_gain
    mix = mix_t.T
    both = mix + mix_t
    half_gain = 0.5 * kernel_gain
    sym = diag * gram + half_gain * both
    outer = (diag * diag) * gram + (diag * kernel_gain) * both + (kernel_gain * kernel_gain) * quad
    curv = diag * gram + kernel_gain * mix
    eye = lax.broadcasted_iota(jnp.int32, (size, size), 0) == lax.broadcasted_iota(jnp.int32, (size, size), 1)
    on_diag = jnp.where(eye, sym, 0.0)
    by_col = lax.rsqrt(jnp.sum(on_diag, axis=0, keepdims=True))
    by_row = lax.rsqrt(jnp.sum(on_diag, axis=1, keepdims=True))
    unit = sym * by_row * by_col
    parts = negated_inverse([unit[8 * i : 8 * i + 8, :] for i in range(size // 8)], size)
    minus_inverse = jnp.concatenate(parts, axis=0) * by_row * by_col
    step_t = -exact_dot(gram, minus_inverse)
    correction_t = exact_dot(curv - exact_dot(step_t, outer), minus_inverse)
    targets = targets_ref[...]
    image = ridge_weight * targets + kernel_gain * (targets.astype(bf16).astype(f32) + z_ref[...])
    residual = targets - exact_dot(step_t, image)
    coef_ref[...] = exact_dot(step_t, targets)
    res_ref[...] = residual
    dir_ref[...] = residual + exact_dot(correction_t, targets)


def flips(size, bit):
    return [(i, i ^ bit) for i in range(size)]


def call(kernel, out_shape, scratch_shapes, operands, limit):
    vmem = pl.BlockSpec(memory_space=pltpu.VMEM)
    return pl.pallas_call(
        kernel,
        out_shape=out_shape,
        in_specs=[vmem] * len(operands),
        out_specs=jax.tree.map(lambda _: vmem, out_shape),
        scratch_shapes=scratch_shapes,
        compiler_params=pltpu.CompilerParams(vmem_limit_bytes=limit),
    )(*operands)


def local(row_size, col_size):
    def run(features, targets):
        return step(features, targets)

    def step(features, targets):
        feat_rows, block = features.shape
        out_rows = targets.shape[0]
        scale = sharpness / feat_rows
        inner_rows = feat_rows + 16

        def flip(axis, bit):
            size = row_size if axis == "row" else col_size

            def send(x):
                return lax.ppermute(x, axis, flips(size, bit))

            return send

        def over_x(x):
            return flip("row", 1)(x)

        def over_y(x):
            return flip("col", col_size // 2)(x)

        def partner(x):
            return flip("col", 1)(x)

        def join(*pieces):
            return jnp.concatenate(pieces, axis=0)

        hops = [("row", 1 << s) for s in reversed(range(1, row_size.bit_length() - 1))]
        hops += [("col", 1 << s) for s in reversed(range(1, col_size.bit_length() - 2))]
        line = join(features, targets.astype(bf16))[None]
        for axis, bit in hops:
            line = join(line, flip(axis, bit)(line))
        other_line = partner(line)
        from_x, from_y = over_x(line), over_y(line)
        near = join(from_x, from_y)
        other_near = partner(near)
        half = line.shape[0] // 2
        far = join(over_x(from_y[:half]), over_y(from_x[half:]))
        other_far = partner(far)

        limit = product_vmem if line.shape[0] <= 4 else None

        def stage(count):
            return [
                ((2 * count * block, inner_rows), bf16),
                ((inner_rows, count * block), bf16),
                ((out_rows, 2 * count * block), bf16),
            ]

        def sums_of(count):
            return ((out_rows, count * block), f32)

        def shapes(entries):
            return tuple(jax.ShapeDtypeStruct(*x) for x in entries)

        n0, n1, n2 = line.shape[0], near.shape[0], far.shape[0]
        left0, right0, panel0, y0 = call(
            first_kernel(feat_rows, scale), shapes(stage(n0) + [sums_of(n0)]), [], [line, other_line], limit
        )
        left1, right1, panel1, y0, y1 = call(
            second_kernel(feat_rows, scale),
            shapes(stage(n1) + [sums_of(n0), sums_of(n1)]),
            [],
            [near, other_near, left0, right0, panel0, y0],
            limit,
        )
        full_left, right_shape, full_panel = stage(n2)
        own_left = ((n2 * block, inner_rows), bf16)
        own_panel = ((out_rows, n2 * block), bf16)
        left2, right2, panel2, y2 = call(
            cover_kernel(feat_rows, scale),
            shapes([own_left, right_shape, own_panel, sums_of(n2)]),
            [],
            [far, left0, panel0, left1, panel1],
            limit,
        )
        z, grams = call(
            third_kernel(feat_rows, scale),
            shapes([((out_rows, block), f32), ((3, out_rows, out_rows), f32)]),
            [pltpu.VMEM(*x) for x in [full_left, full_panel, ((3 * out_rows, 2 * out_rows), f32)]],
            [other_far, left2, right2, panel2, right0, panel0, right1, panel1, y0, y1, y2],
            limit,
        )
        return call(
            solve_kernel,
            tuple(jax.ShapeDtypeStruct(targets.shape, f32) for _ in range(3)),
            [],
            [grams, partner(grams), targets, z],
            solve_vmem,
        )

    return run


def solution(mesh):
    spec = P(None, ("col", "row"))
    return jax.shard_map(
        local(mesh.shape["row"], mesh.shape["col"]),
        mesh=mesh,
        in_specs=(spec, spec),
        out_specs=(spec, spec, spec),
        check_vma=False,
    )
```

time: 42.2 us -> 41.2 us (0.976)
  Pallas kernels: 14.5 us -> 13.2 us
  waiting for transfers between devices: 12.7 us -> 14 us
  starting transfers between devices: 13.1 us -> 12.2 us
    pallas_call x3 -> x5, Pallas kernels: 14.5 us -> 13.2 us  [call(): pl.pallas_call(kernel, out_shape=out_shape, in_specs=[vmem] * len(operand...]
    ppermute x11 -> x10, waiting for transfers between devices: 12.7 us -> 14 us  [send(): return lax.ppermute(x, axis, flips(size, bit))]
    ppermute x11 -> x10, starting transfers between devices: 13.1 us -> 12.2 us  [send(): return lax.ppermute(x, axis, flips(size, bit))]
  transfers between devices with their start and end apart: 11 -> 10, of which waited for: 7 -> 6; matrix products, arithmetic and copies ran while one was open for 0% -> 0% of each run, Pallas kernels for 10% -> 14%
where the time goes in v1:
time: 41.2 us; the launch traced here: 41 us
  waiting for transfers between devices  14 us (34%)
  Pallas kernels  13.2 us (32%)
  starting transfers between devices  12.2 us (30%)
  other arithmetic  0.89 us (2%)
  between operations  0.77 us (2%)
    ppermute x10, waiting for transfers between devices, send(): return lax.ppermute(x, axis, flips(size, bit))  14 us
    pallas_call x5, Pallas kernels, call(): pl.pallas_call(kernel, out_shape=out_shape, in_specs=[vmem] * len(operand...  13.2 us
    ppermute x10, starting transfers between devices, send(): return lax.ppermute(x, axis, flips(size, bit))  12.2 us
    convert_element_type x1, other arithmetic, step(): line = join(features, targets.astype(bf16))[None]  0.85 us
  transfers between devices with their start and end apart: 10, of which 6 were waited for; matrix products, arithmetic and copies ran while one was open for 0% of the time, Pallas kernels for 14%

profile of v1, /device:TPU:0, one launch (start us, length us, event | category | flops | bytes accessed | tf_op | source)
XLA Modules:
  0.0 41.0 jit_solution(10658759330414736404)
XLA Ops:
  0.6 0.0 copy-start.1
  0.6 0.9 %convert_element_type.3 = bf16[128,128]{1,0:T(8,128)(2,1)S(1)} convert(f32[128,128]{1,0:T(8,128)} %targets_ref.1) | non-fusion elementwise | flops 16384 | bytes 98304 | tf_op jit(solution)/shard_map/convert_element_type | solution.py:305
  1.5 0.0 copy-done.1
  1.5 4.1 %collective-permute-start = (bf16[1,192,128]{2,1,0:T(8,128)(2,1)S(1)}, bf16[1,192,128]{2,1,0:T(8,128)(2,1)S(1)}, u32[]{:S(2)}, u32[]{:S(2)}) collective-permute-start(bf16[1,192,128]{2,1,0:T(8,128)(2,1)S(1)} %maximum_bitcast_fusion), channel_id=1, source_target_pairs={{0,16},{4,20},{8,24},{12,28},{16,0},{20,4},{24,8},{28,12},{1,17},{... | collective-permute-start | bytes 147464 | tf_op jit(solution)/shard_map/ppermute | solution.py:287
  5.6 2.6 %collective-permute-done = bf16[1,192,128]{2,1,0:T(8,128)(2,1)S(1)} collective-permute-done((bf16[1,192,128]{2,1,0:T(8,128)(2,1)S(1)}, bf16[1,192,128]{2,1,0:T(8,128)(2,1)S(1)}, u32[]{:S(2)}, u32[]{:S(2)}) %collective-permute-start) | collective-permute-done | bytes 49184 | tf_op jit(solution)/shard_map/ppermute | solution.py:287
  8.2 1.4 %collective-permute-start.1 = (bf16[2,192,128]{2,1,0:T(8,128)(2,1)S(1)}, bf16[2,192,128]{2,1,0:T(8,128)(2,1)S(1)}, u32[]{:S(2)}, u32[]{:S(2)}) collective-permute-start(bf16[2,192,128]{2,1,0:T(8,128)(2,1)S(1)} %pad_maximum_fusion.1), channel_id=1, source_target_pairs={{0,8},{4,12},{8,0},{12,4},{16,24},{20,28},{24,16},{28,20},{1,9},{5... | collective-permute-start | bytes 294920 | tf_op jit(solution)/shard_map/ppermute | solution.py:287
  9.7 3.2 %collective-permute-done.1 = bf16[2,192,128]{2,1,0:T(8,128)(2,1)S(1)} collective-permute-done((bf16[2,192,128]{2,1,0:T(8,128)(2,1)S(1)}, bf16[2,192,128]{2,1,0:T(8,128)(2,1)S(1)}, u32[]{:S(2)}, u32[]{:S(2)}) %collective-permute-start.1) | collective-permute-done | bytes 98336 | tf_op jit(solution)/shard_map/ppermute | solution.py:287
  12.9 1.8 %collective-permute-start.4 = (bf16[4,192,128]{2,1,0:T(8,128)(2,1)S(1)}, bf16[4,192,128]{2,1,0:T(8,128)(2,1)S(1)}, u32[]{:S(2)}, u32[]{:S(2)}) collective-permute-start(bf16[4,192,128]{2,1,0:T(8,128)(2,1)S(1)} %pad_maximum_fusion.own), channel_id=1, source_target_pairs={{0,4},{4,0},{8,12},{12,8},{16,20},{20,16},{24,28},{28,24},{1,5},{5... | collective-permute-start | bytes 589832 | tf_op jit(solution)/shard_map/ppermute | solution.py:287
  14.7 1.5 %collective-permute-start.2 = (bf16[4,192,128]{2,1,0:T(8,128)(2,1)S(1)}, bf16[4,192,128]{2,1,0:T(8,128)(2,1)S(1)}, u32[]{:S(2)}, u32[]{:S(2)}) collective-permute-start(bf16[4,192,128]{2,1,0:T(8,128)(2,1)S(1)} %pad_maximum_fusion.own), channel_id=1, source_target_pairs={{0,2},{1,3},{2,0},{3,1},{4,6},{5,7},{6,4},{7,5},{8,10},{9,11},{10,... | collective-permute-start | bytes 589832 | tf_op jit(solution)/shard_map/ppermute | solution.py:287
  16.2 0.0 collective-permute-start.7
  16.2 2.4 %collective-permute-done.4 = bf16[4,192,128]{2,1,0:T(8,128)(2,1)S(1)} collective-permute-done((bf16[4,192,128]{2,1,0:T(8,128)(2,1)S(1)}, bf16[4,192,128]{2,1,0:T(8,128)(2,1)S(1)}, u32[]{:S(2)}, u32[]{:S(2)}) %collective-permute-start.4) | collective-permute-done | bytes 196640 | tf_op jit(solution)/shard_map/ppermute | solution.py:287
  18.7 1.8 %collective-permute-start.5 = (bf16[2,192,128]{2,1,0:T(8,128)(2,1)S(1)}, bf16[2,192,128]{2,1,0:T(8,128)(2,1)S(1)}, u32[]{:S(2)}, u32[]{:S(2)}) collective-permute-start(bf16[2,192,128]{2,1,0:T(8,128)(2,1)S(1)} %slice.9), channel_id=1, source_target_pairs={{0,2},{1,3},{2,0},{3,1},{4,6},{5,7},{6,4},{7,5},{8,10},{9,11},{10,... | collective-permute-start | bytes 294920 | tf_op jit(solution)/shard_map/ppermute | solution.py:287
  20.5 0.9 %collective-permute-done.2 = bf16[4,192,128]{2,1,0:T(8,128)(2,1)S(1)} collective-permute-done((bf16[4,192,128]{2,1,0:T(8,128)(2,1)S(1)}, bf16[4,192,128]{2,1,0:T(8,128)(2,1)S(1)}, u32[]{:S(2)}, u32[]{:S(2)}) %collective-permute-start.2) | collective-permute-done | bytes 196640 | tf_op jit(solution)/shard_map/ppermute | solution.py:287
  21.4 0.8 %collective-permute-start.3 = (bf16[2,192,128]{2,1,0:T(8,128)(2,1)S(1)}, bf16[2,192,128]{2,1,0:T(8,128)(2,1)S(1)}, u32[]{:S(2)}, u32[]{:S(2)}) collective-permute-start(bf16[2,192,128]{2,1,0:T(8,128)(2,1)S(1)} %slice.8), channel_id=1, source_target_pairs={{0,4},{4,0},{8,12},{12,8},{16,20},{20,16},{24,28},{28,24},{1,5},{5... | collective-permute-start | bytes 294920 | tf_op jit(solution)/shard_map/ppermute | solution.py:287
  22.2 0.1 collective-permute-start.8
  22.3 3.7 %collective-permute-done.3 = bf16[2,192,128]{2,1,0:T(8,128)(2,1)S(1)} collective-permute-done((bf16[2,192,128]{2,1,0:T(8,128)(2,1)S(1)}, bf16[2,192,128]{2,1,0:T(8,128)(2,1)S(1)}, u32[]{:S(2)}, u32[]{:S(2)}) %collective-permute-start.3) | collective-permute-done | bytes 98336 | tf_op jit(solution)/shard_map/ppermute | solution.py:287
  26.1 0.0 collective-permute-done.5
  26.1 0.1 collective-permute-start.6
  26.2 0.0 collective-permute-done.7.other
  26.2 0.7 %shard_map.49 = (bf16[1024,80]{1,0:T(8,128)(2,1)S(1)}, bf16[80,512]{1,0:T(8,128)(2,1)S(1)}, bf16[128,1024]{1,0:T(8,128)(2,1)S(1)}, f32[128,512]{1,0:T(8,128)S(1)}) custom-call(bf16[4,192,128]{2,1,0:T(8,128)(2,1)S(1)} %pad_maximum_fusion.own, bf16[4,192,128]{2,1,0:T(8,128)(2,1)S(1)} %collective-permute-done.7.other), custom_call_target="tpu_custom_call" | custom-call | tf_op jit(solution)/shard_map/pallas_call | solution.py:263
  26.9 0.0 collective-permute-done.8.other
  26.9 3.6 %shard_map.50 = (bf16[2048,80]{1,0:T(8,128)(2,1)S(1)}, bf16[80,1024]{1,0:T(8,128)(2,1)S(1)}, bf16[128,2048]{1,0:T(8,128)(2,1)S(1)}, f32[128,512]{1,0:T(8,128)S(1)}, f32[128,1024]{1,0:T(8,128)S(1)}) custom-call(bf16[8,192,128]{2,1,0:T(8,128)(2,1)S(1)} %constant_dynamic-update-slice_fusion.2.own, bf16[8,192,128]{2,1,0:T(8,128)(2,1)S(1)} %collective-permute-done.8.other, ...), custom_call_target="tpu_custom_call" | custom-call | tf_op jit(solution)/shard_map/pallas_call | solution.py:263
  30.4 1.4 %shard_map.51 = (bf16[512,80]{1,0:T(8,128)(2,1)S(1)}, bf16[80,512]{1,0:T(8,128)(2,1)S(1)}, bf16[128,512]{1,0:T(8,128)(2,1)S(1)}, f32[128,512]{1,0:T(8,128)S(1)}) custom-call(bf16[4,192,128]{2,1,0:T(8,128)(2,1)S(1)} %constant_dynamic-update-slice_fusion.own, bf16[1024,80]{1,0:T(8,128)(2,1)S(1)} %get-tuple-element.18.left0, ...), custom_call_target="tpu_custom_call" | custom-call | tf_op jit(solution)/shard_map/pallas_call | solution.py:263
  31.9 0.0 collective-permute-done.6.other
  31.9 0.0 copy-start
  31.9 2.8 %shard_map.52 = (f32[128,128]{1,0:T(8,128)S(1)}, f32[3,128,128]{2,1,0:T(8,128)S(1)}) custom-call(bf16[4,192,128]{2,1,0:T(8,128)(2,1)S(1)} %collective-permute-done.6.other, bf16[512,80]{1,0:T(8,128)(2,1)S(1)} %get-tuple-element.24.refs_0_, bf16[80,512]{1,0:T(8,128)(2,1)S(1)} %get-tuple-element.25.refs_1_, bf16[128,512]{1,0:T(8,128)(2,1)S(1)} %get-tuple-element.26.refs_2_, ...), custom_call_target="tpu_custom_call" | custom-call | tf_op jit(solution)/shard_map/pallas_call | solution.py:263
  34.7 0.6 %collective-permute-start.9 = (f32[3,128,128]{2,1,0:T(8,128)S(1)}, f32[3,128,128]{2,1,0:T(8,128)S(1)}, u32[]{:S(2)}, u32[]{:S(2)}) collective-permute-start(f32[3,128,128]{2,1,0:T(8,128)S(1)} %get-tuple-element.31.mine), channel_id=1, source_target_pairs={{0,1},{1,0},{2,3},{3,2},{4,5},{5,4},{6,7},{7,6},{8,9},{9,8},{10,11... | collective-permute-start | bytes 589832 | tf_op jit(solution)/shard_map/ppermute | solution.py:287
  35.3 1.1 %collective-permute-done.9.other = f32[3,128,128]{2,1,0:T(8,128)S(1)} collective-permute-done((f32[3,128,128]{2,1,0:T(8,128)S(1)}, f32[3,128,128]{2,1,0:T(8,128)S(1)}, u32[]{:S(2)}, u32[]{:S(2)}) %collective-permute-start.9) | collective-permute-done | bytes 196640 | tf_op jit(solution)/shard_map/ppermute | solution.py:287
  36.3 0.0 copy-done
  36.3 4.7 %shard_map.53 = (f32[128,128]{1,0:T(8,128)}, f32[128,128]{1,0:T(8,128)}, f32[128,128]{1,0:T(8,128)}) custom-call(f32[3,128,128]{2,1,0:T(8,128)S(1)} %get-tuple-element.31.mine, f32[3,128,128]{2,1,0:T(8,128)S(1)} %collective-permute-done.9.other, f32[128,128]{1,0:T(8,128)S(1)} %copy-done, f32[128,128]{1,0:T(8,128)S(1)} %get-tuple-element.32.z_ref), custom_call_target="tpu_custom_call" | custom-call | tf_op jit(solution)/shard_map/pallas_call | solution.py:263
  (9 shorter events, 0.1 us)
Async XLA Ops:
  0.6 0.9 %copy-start.1 = (bf16[64,128]{1,0:T(8,128)(2,1)S(1)}, bf16[64,128]{1,0:T(8,128)(2,1)}, u32[]{:S(2)}) copy-start(bf16[64,128]{1,0:T(8,128)(2,1)} %param.2) | copy-start | bytes 49156
  1.5 6.7 %collective-permute-start = (bf16[1,192,128]{2,1,0:T(8,128)(2,1)S(1)}, bf16[1,192,128]{2,1,0:T(8,128)(2,1)S(1)}, u32[]{:S(2)}, u32[]{:S(2)}) collective-permute-start(bf16[1,192,128]{2,1,0:T(8,128)(2,1)S(1)} %maximum_bitcast_fusion), channel_id=1, source_target_pairs={{0,16},{4,20},{8,24},{12,28},{16,0},{20,4},{24,8},{28,12},{1,17},{... | collective-permute-start | bytes 147464 | tf_op jit(solution)/shard_map/ppermute | solution.py:287
  8.2 4.7 %collective-permute-start.1 = (bf16[2,192,128]{2,1,0:T(8,128)(2,1)S(1)}, bf16[2,192,128]{2,1,0:T(8,128)(2,1)S(1)}, u32[]{:S(2)}, u32[]{:S(2)}) collective-permute-start(bf16[2,192,128]{2,1,0:T(8,128)(2,1)S(1)} %pad_maximum_fusion.1), channel_id=1, source_target_pairs={{0,8},{4,12},{8,0},{12,4},{16,24},{20,28},{24,16},{28,20},{1,9},{5... | collective-permute-start | bytes 294920 | tf_op jit(solution)/shard_map/ppermute | solution.py:287
  12.9 5.7 %collective-permute-start.4 = (bf16[4,192,128]{2,1,0:T(8,128)(2,1)S(1)}, bf16[4,192,128]{2,1,0:T(8,128)(2,1)S(1)}, u32[]{:S(2)}, u32[]{:S(2)}) collective-permute-start(bf16[4,192,128]{2,1,0:T(8,128)(2,1)S(1)} %pad_maximum_fusion.own), channel_id=1, source_target_pairs={{0,4},{4,0},{8,12},{12,8},{16,20},{20,16},{24,28},{28,24},{1,5},{5... | collective-permute-start | bytes 589832 | tf_op jit(solution)/shard_map/ppermute | solution.py:287
  14.7 6.6 %collective-permute-start.2 = (bf16[4,192,128]{2,1,0:T(8,128)(2,1)S(1)}, bf16[4,192,128]{2,1,0:T(8,128)(2,1)S(1)}, u32[]{:S(2)}, u32[]{:S(2)}) collective-permute-start(bf16[4,192,128]{2,1,0:T(8,128)(2,1)S(1)} %pad_maximum_fusion.own), channel_id=1, source_target_pairs={{0,2},{1,3},{2,0},{3,1},{4,6},{5,7},{6,4},{7,5},{8,10},{9,11},{10,... | collective-permute-start | bytes 589832 | tf_op jit(solution)/shard_map/ppermute | solution.py:287
  16.2 9.9 %collective-permute-start.7 = (bf16[4,192,128]{2,1,0:T(8,128)(2,1)S(1)}, bf16[4,192,128]{2,1,0:T(8,128)(2,1)S(1)}, u32[]{:S(2)}, u32[]{:S(2)}) collective-permute-start(bf16[4,192,128]{2,1,0:T(8,128)(2,1)S(1)} %pad_maximum_fusion.own), channel_id=1, source_target_pairs={{0,1},{1,0},{2,3},{3,2},{4,5},{5,4},{6,7},{7,6},{8,9},{9,8},{10,11... | collective-permute-start | bytes 589832 | tf_op jit(solution)/shard_map/ppermute | solution.py:287
  18.7 7.4 %collective-permute-start.5 = (bf16[2,192,128]{2,1,0:T(8,128)(2,1)S(1)}, bf16[2,192,128]{2,1,0:T(8,128)(2,1)S(1)}, u32[]{:S(2)}, u32[]{:S(2)}) collective-permute-start(bf16[2,192,128]{2,1,0:T(8,128)(2,1)S(1)} %slice.9), channel_id=1, source_target_pairs={{0,2},{1,3},{2,0},{3,1},{4,6},{5,7},{6,4},{7,5},{8,10},{9,11},{10,... | collective-permute-start | bytes 294920 | tf_op jit(solution)/shard_map/ppermute | solution.py:287
  21.4 4.7 %collective-permute-start.3 = (bf16[2,192,128]{2,1,0:T(8,128)(2,1)S(1)}, bf16[2,192,128]{2,1,0:T(8,128)(2,1)S(1)}, u32[]{:S(2)}, u32[]{:S(2)}) collective-permute-start(bf16[2,192,128]{2,1,0:T(8,128)(2,1)S(1)} %slice.8), channel_id=1, source_target_pairs={{0,4},{4,0},{8,12},{12,8},{16,20},{20,16},{24,28},{28,24},{1,5},{5... | collective-permute-start | bytes 294920 | tf_op jit(solution)/shard_map/ppermute | solution.py:287
  22.2 4.6 %collective-permute-start.8 = (bf16[8,192,128]{2,1,0:T(8,128)(2,1)S(1)}, bf16[8,192,128]{2,1,0:T(8,128)(2,1)S(1)}, u32[]{:S(2)}, u32[]{:S(2)}) collective-permute-start(bf16[8,192,128]{2,1,0:T(8,128)(2,1)S(1)} %constant_dynamic-update-slice_fusion.2.own), channel_id=1, source_target_pairs={{0,1},{1,0},{2,3},{3,2},{4,5},{5,4},{6,7},{7,6},{8,9},{9,8},{10,11... | collective-permute-start | bytes 1179656 | tf_op jit(solution)/shard_map/ppermute | solution.py:287
  26.1 5.8 %collective-permute-start.6 = (bf16[4,192,128]{2,1,0:T(8,128)(2,1)S(1)}, bf16[4,192,128]{2,1,0:T(8,128)(2,1)S(1)}, u32[]{:S(2)}, u32[]{:S(2)}) collective-permute-start(bf16[4,192,128]{2,1,0:T(8,128)(2,1)S(1)} %constant_dynamic-update-slice_fusion.own), channel_id=1, source_target_pairs={{0,1},{1,0},{2,3},{3,2},{4,5},{5,4},{6,7},{7,6},{8,9},{9,8},{10,11... | collective-permute-start | bytes 589832 | tf_op jit(solution)/shard_map/ppermute | solution.py:287
  31.9 4.4 %copy-start = (f32[128,128]{1,0:T(8,128)S(1)}, f32[128,128]{1,0:T(8,128)}, u32[]{:S(2)}) copy-start(f32[128,128]{1,0:T(8,128)} %targets_ref.1) | copy-start | bytes 196612
  34.7 1.6 %collective-permute-start.9 = (f32[3,128,128]{2,1,0:T(8,128)S(1)}, f32[3,128,128]{2,1,0:T(8,128)S(1)}, u32[]{:S(2)}, u32[]{:S(2)}) collective-permute-start(f32[3,128,128]{2,1,0:T(8,128)S(1)} %get-tuple-element.31.mine), channel_id=1, source_target_pairs={{0,1},{1,0},{2,3},{3,2},{4,5},{5,4},{6,7},{7,6},{8,9},{9,8},{10,11... | collective-permute-start | bytes 589832 | tf_op jit(solution)/shard_map/ppermute | solution.py:287

commit v2 on v1

--- a/solution.py
+++ b/solution.py
@@ -147,11 +147,8 @@
                         z_ref[...] = z[:, :block]
 
                     put() if is_first is True else pl.when(is_first)(put)
-                high = z.astype(bf16)
-                low = (z - high.astype(f32)).astype(bf16)
-                rhs = jnp.concatenate([own_panel, high], axis=0)
-                lhs = jnp.concatenate([rhs, low], axis=0)
-                sums[...] += lax.dot_general(lhs, rhs, (((1,), (1,)), ((), ())), preferred_element_type=f32)
+                both = jnp.concatenate([own_panel, z.astype(bf16)], axis=0)
+                sums[...] += lax.dot_general(both, both, (((1,), (1,)), ((), ())), preferred_element_type=f32)
 
             over_columns(right_of.shape[1], work)
 
@@ -159,10 +156,9 @@
         add_columns(right1, panel1, y1, False)
         add_columns(right, panel, y2, False)
         r = panel.shape[0]
-        cross = sums[2 * r :, r:]
         gram_ref[0] = sums[:r, :r]
-        gram_ref[1] = sums[r : 2 * r, :r] + sums[2 * r :, :r]
-        gram_ref[2] = sums[r : 2 * r, r:] + cross + cross.T
+        gram_ref[1] = sums[r:, :r]
+        gram_ref[2] = sums[r:, r:]
 
     return body
 
@@ -306,11 +302,13 @@
         for axis, bit in hops:
             line = join(line, flip(axis, bit)(line))
         other_line = partner(line)
-        from_x, from_y = over_x(line), over_y(line)
-        near = join(from_x, from_y)
+        half = line.shape[0] // 2
+        early_y = over_y(line[:half])
+        from_x, late_y = over_x(line), over_y(line[half:])
+        far_x = over_x(early_y)
+        near = join(from_x, early_y, late_y)
         other_near = partner(near)
-        half = line.shape[0] // 2
-        far = join(over_x(from_y[:half]), over_y(from_x[half:]))
+        far = join(far_x, over_y(from_x[half:]))
         other_far = partner(far)
 
         limit = product_vmem if line.shape[0] <= 4 else None
@@ -352,7 +350,7 @@
         z, grams = call(
             third_kernel(feat_rows, scale),
             shapes([((out_rows, block), f32), ((3, out_rows, out_rows), f32)]),
-            [pltpu.VMEM(*x) for x in [full_left, full_panel, ((3 * out_rows, 2 * out_rows), f32)]],
+            [pltpu.VMEM(*x) for x in [full_left, full_panel, ((2 * out_rows, 2 * out_rows), f32)]],
             [other_far, left2, right2, panel2, right0, panel0, right1, panel1, y0, y1, y2],
             limit,
         )

time: 41.2 us -> 41.7 us (1.012)
  waiting for transfers between devices: 14 us -> 14.8 us
    ppermute x10 -> x11, waiting for transfers between devices: 14 us -> 14.8 us  [send(): return lax.ppermute(x, axis, flips(size, bit))]
    ppermute x10 -> x11, starting transfers between devices: 12.2 us -> 12.1 us  [send(): return lax.ppermute(x, axis, flips(size, bit))]
  transfers between devices with their start and end apart: 10 -> 11, of which waited for: 6 -> 7; matrix products, arithmetic and copies ran while one was open for 0% -> 0% of each run, Pallas kernels for 14% -> 14%
where the time goes in v2:
time: 41.7 us; the launch traced here: 41.5 us
  waiting for transfers between devices  14.8 us (35%)
  Pallas kernels  12.9 us (31%)
  starting transfers between devices  12.1 us (29%)
  other arithmetic  0.89 us (2%)
  between operations  0.76 us (2%)
    ppermute x11, waiting for transfers between devices, send(): return lax.ppermute(x, axis, flips(size, bit))  14.8 us
    pallas_call x5, Pallas kernels, call(): pl.pallas_call(kernel, out_shape=out_shape, in_specs=[vmem] * len(operand...  12.9 us
    ppermute x11, starting transfers between devices, send(): return lax.ppermute(x, axis, flips(size, bit))  12.1 us
    convert_element_type x1, other arithmetic, step(): line = join(features, targets.astype(bf16))[None]  0.85 us
  transfers between devices with their start and end apart: 11, of which 7 were waited for; matrix products, arithmetic and copies ran while one was open for 0% of the time, Pallas kernels for 14%

profile of v2, /device:TPU:0, one launch (start us, length us, event | category | flops | bytes accessed | tf_op | source)
XLA Modules:
  0.0 41.5 jit_solution(17473047950578248446)
XLA Ops:
  0.6 0.0 copy-start.1
  0.6 0.9 %convert_element_type.3 = bf16[128,128]{1,0:T(8,128)(2,1)S(1)} convert(f32[128,128]{1,0:T(8,128)} %targets_ref.1) | non-fusion elementwise | flops 16384 | bytes 98304 | tf_op jit(solution)/shard_map/convert_element_type | solution.py:301
  1.5 0.0 copy-done.1
  1.5 4.1 %collective-permute-start = (bf16[1,192,128]{2,1,0:T(8,128)(2,1)S(1)}, bf16[1,192,128]{2,1,0:T(8,128)(2,1)S(1)}, u32[]{:S(2)}, u32[]{:S(2)}) collective-permute-start(bf16[1,192,128]{2,1,0:T(8,128)(2,1)S(1)} %maximum_bitcast_fusion), channel_id=1, source_target_pairs={{0,16},{4,20},{8,24},{12,28},{16,0},{20,4},{24,8},{28,12},{1,17},{... | collective-permute-start | bytes 147464 | tf_op jit(solution)/shard_map/ppermute | solution.py:283
  5.6 2.6 %collective-permute-done = bf16[1,192,128]{2,1,0:T(8,128)(2,1)S(1)} collective-permute-done((bf16[1,192,128]{2,1,0:T(8,128)(2,1)S(1)}, bf16[1,192,128]{2,1,0:T(8,128)(2,1)S(1)}, u32[]{:S(2)}, u32[]{:S(2)}) %collective-permute-start) | collective-permute-done | bytes 49184 | tf_op jit(solution)/shard_map/ppermute | solution.py:283
  8.2 1.4 %collective-permute-start.3 = (bf16[2,192,128]{2,1,0:T(8,128)(2,1)S(1)}, bf16[2,192,128]{2,1,0:T(8,128)(2,1)S(1)}, u32[]{:S(2)}, u32[]{:S(2)}) collective-permute-start(bf16[2,192,128]{2,1,0:T(8,128)(2,1)S(1)} %pad_maximum_fusion.1), channel_id=1, source_target_pairs={{0,8},{4,12},{8,0},{12,4},{16,24},{20,28},{24,16},{28,20},{1,9},{5... | collective-permute-start | bytes 294920 | tf_op jit(solution)/shard_map/ppermute | solution.py:283
  9.7 3.2 %collective-permute-done.3 = bf16[2,192,128]{2,1,0:T(8,128)(2,1)S(1)} collective-permute-done((bf16[2,192,128]{2,1,0:T(8,128)(2,1)S(1)}, bf16[2,192,128]{2,1,0:T(8,128)(2,1)S(1)}, u32[]{:S(2)}, u32[]{:S(2)}) %collective-permute-start.3) | collective-permute-done | bytes 98336 | tf_op jit(solution)/shard_map/ppermute | solution.py:283
  12.9 1.8 %collective-permute-start.4 = (bf16[4,192,128]{2,1,0:T(8,128)(2,1)S(1)}, bf16[4,192,128]{2,1,0:T(8,128)(2,1)S(1)}, u32[]{:S(2)}, u32[]{:S(2)}) collective-permute-start(bf16[4,192,128]{2,1,0:T(8,128)(2,1)S(1)} %pad_maximum_fusion.own), channel_id=1, source_target_pairs={{0,4},{4,0},{8,12},{12,8},{16,20},{20,16},{24,28},{28,24},{1,5},{5... | collective-permute-start | bytes 589832 | tf_op jit(solution)/shard_map/ppermute | solution.py:283
  14.7 1.5 %collective-permute-start.1 = (bf16[2,192,128]{2,1,0:T(8,128)(2,1)S(1)}, bf16[2,192,128]{2,1,0:T(8,128)(2,1)S(1)}, u32[]{:S(2)}, u32[]{:S(2)}) collective-permute-start(bf16[2,192,128]{2,1,0:T(8,128)(2,1)S(1)} %pad_maximum_fusion.1), channel_id=1, source_target_pairs={{0,2},{1,3},{2,0},{3,1},{4,6},{5,7},{6,4},{7,5},{8,10},{9,11},{10,... | collective-permute-start | bytes 294920 | tf_op jit(solution)/shard_map/ppermute | solution.py:283
  16.2 0.0 collective-permute-start.7
  16.2 0.5 %collective-permute-start.8 = (bf16[2,192,128]{2,1,0:T(8,128)(2,1)S(1)}, bf16[2,192,128]{2,1,0:T(8,128)(2,1)S(1)}, u32[]{:S(2)}, u32[]{:S(2)}) collective-permute-start(bf16[2,192,128]{2,1,0:T(8,128)(2,1)S(1)} %collective-permute-done.3), channel_id=1, source_target_pairs={{0,2},{1,3},{2,0},{3,1},{4,6},{5,7},{6,4},{7,5},{8,10},{9,11},{10,... | collective-permute-start | bytes 294920 | tf_op jit(solution)/shard_map/ppermute | solution.py:283
  16.7 2.6 %collective-permute-done.1 = bf16[2,192,128]{2,1,0:T(8,128)(2,1)S(1)} collective-permute-done((bf16[2,192,128]{2,1,0:T(8,128)(2,1)S(1)}, bf16[2,192,128]{2,1,0:T(8,128)(2,1)S(1)}, u32[]{:S(2)}, u32[]{:S(2)}) %collective-permute-start.1) | collective-permute-done | bytes 98336 | tf_op jit(solution)/shard_map/ppermute | solution.py:283
  19.4 0.4 %collective-permute-start.2 = (bf16[2,192,128]{2,1,0:T(8,128)(2,1)S(1)}, bf16[2,192,128]{2,1,0:T(8,128)(2,1)S(1)}, u32[]{:S(2)}, u32[]{:S(2)}) collective-permute-start(bf16[2,192,128]{2,1,0:T(8,128)(2,1)S(1)} %collective-permute-done.1), channel_id=1, source_target_pairs={{0,4},{4,0},{8,12},{12,8},{16,20},{20,16},{24,28},{28,24},{1,5},{5... | collective-permute-start | bytes 294920 | tf_op jit(solution)/shard_map/ppermute | solution.py:283
  19.8 0.0 collective-permute-done.4
  19.8 1.6 %collective-permute-done.8 = bf16[2,192,128]{2,1,0:T(8,128)(2,1)S(1)} collective-permute-done((bf16[2,192,128]{2,1,0:T(8,128)(2,1)S(1)}, bf16[2,192,128]{2,1,0:T(8,128)(2,1)S(1)}, u32[]{:S(2)}, u32[]{:S(2)}) %collective-permute-start.8) | collective-permute-done | bytes 98336 | tf_op jit(solution)/shard_map/ppermute | solution.py:283
  21.5 0.1 collective-permute-start.9
  21.6 1.6 %collective-permute-start.5 = (bf16[2,192,128]{2,1,0:T(8,128)(2,1)S(1)}, bf16[2,192,128]{2,1,0:T(8,128)(2,1)S(1)}, u32[]{:S(2)}, u32[]{:S(2)}) collective-permute-start(bf16[2,192,128]{2,1,0:T(8,128)(2,1)S(1)} %slice.4), channel_id=1, source_target_pairs={{0,2},{1,3},{2,0},{3,1},{4,6},{5,7},{6,4},{7,5},{8,10},{9,11},{10,... | collective-permute-start | bytes 294920 | tf_op jit(solution)/shard_map/ppermute | solution.py:283
  23.1 0.9 %collective-permute-done.2 = bf16[2,192,128]{2,1,0:T(8,128)(2,1)S(1)} collective-permute-done((bf16[2,192,128]{2,1,0:T(8,128)(2,1)S(1)}, bf16[2,192,128]{2,1,0:T(8,128)(2,1)S(1)}, u32[]{:S(2)}, u32[]{:S(2)}) %collective-permute-start.2) | collective-permute-done | bytes 98336 | tf_op jit(solution)/shard_map/ppermute | solution.py:283
  24.0 2.8 %collective-permute-done.5 = bf16[2,192,128]{2,1,0:T(8,128)(2,1)S(1)} collective-permute-done((bf16[2,192,128]{2,1,0:T(8,128)(2,1)S(1)}, bf16[2,192,128]{2,1,0:T(8,128)(2,1)S(1)}, u32[]{:S(2)}, u32[]{:S(2)}) %collective-permute-start.5) | collective-permute-done | bytes 98336 | tf_op jit(solution)/shard_map/ppermute | solution.py:283
  26.8 0.1 collective-permute-start.6
  26.9 0.0 collective-permute-done.7.other
  26.9 0.7 %shard_map.49 = (bf16[1024,80]{1,0:T(8,128)(2,1)S(1)}, bf16[80,512]{1,0:T(8,128)(2,1)S(1)}, bf16[128,1024]{1,0:T(8,128)(2,1)S(1)}, f32[128,512]{1,0:T(8,128)S(1)}) custom-call(bf16[4,192,128]{2,1,0:T(8,128)(2,1)S(1)} %pad_maximum_fusion.own, bf16[4,192,128]{2,1,0:T(8,128)(2,1)S(1)} %collective-permute-done.7.other), custom_call_target="tpu_custom_call" | custom-call | tf_op jit(solution)/shard_map/pallas_call | solution.py:259
  27.6 0.0 collective-permute-done.9.other
  27.6 3.6 %shard_map.50 = (bf16[2048,80]{1,0:T(8,128)(2,1)S(1)}, bf16[80,1024]{1,0:T(8,128)(2,1)S(1)}, bf16[128,2048]{1,0:T(8,128)(2,1)S(1)}, f32[128,512]{1,0:T(8,128)S(1)}, f32[128,1024]{1,0:T(8,128)S(1)}) custom-call(bf16[8,192,128]{2,1,0:T(8,128)(2,1)S(1)} %constant_dynamic-update-slice_fusion.2.own, bf16[8,192,128]{2,1,0:T(8,128)(2,1)S(1)} %collective-permute-done.9.other, ...), custom_call_target="tpu_custom_call" | custom-call | tf_op jit(solution)/shard_map/pallas_call | solution.py:259
  31.2 1.4 %shard_map.51 = (bf16[512,80]{1,0:T(8,128)(2,1)S(1)}, bf16[80,512]{1,0:T(8,128)(2,1)S(1)}, bf16[128,512]{1,0:T(8,128)(2,1)S(1)}, f32[128,512]{1,0:T(8,128)S(1)}) custom-call(bf16[4,192,128]{2,1,0:T(8,128)(2,1)S(1)} %constant_dynamic-update-slice_fusion.own, bf16[1024,80]{1,0:T(8,128)(2,1)S(1)} %get-tuple-element.18.left0, ...), custom_call_target="tpu_custom_call" | custom-call | tf_op jit(solution)/shard_map/pallas_call | solution.py:259
  32.6 0.0 collective-permute-done.6.other
  32.6 0.0 copy-start
  32.6 2.5 %shard_map.52 = (f32[128,128]{1,0:T(8,128)S(1)}, f32[3,128,128]{2,1,0:T(8,128)S(1)}) custom-call(bf16[4,192,128]{2,1,0:T(8,128)(2,1)S(1)} %collective-permute-done.6.other, bf16[512,80]{1,0:T(8,128)(2,1)S(1)} %get-tuple-element.24.refs_0_, bf16[80,512]{1,0:T(8,128)(2,1)S(1)} %get-tuple-element.25.refs_1_, bf16[128,512]{1,0:T(8,128)(2,1)S(1)} %get-tuple-element.26.refs_2_, ...), custom_call_target="tpu_custom_call" | custom-call | tf_op jit(solution)/shard_map/pallas_call | solution.py:259
  35.2 0.6 %collective-permute-start.10 = (f32[3,128,128]{2,1,0:T(8,128)S(1)}, f32[3,128,128]{2,1,0:T(8,128)S(1)}, u32[]{:S(2)}, u32[]{:S(2)}) collective-permute-start(f32[3,128,128]{2,1,0:T(8,128)S(1)} %get-tuple-element.31.mine), channel_id=1, source_target_pairs={{0,1},{1,0},{2,3},{3,2},{4,5},{5,4},{6,7},{7,6},{8,9},{9,8},{10,11... | collective-permute-start | bytes 589832 | tf_op jit(solution)/shard_map/ppermute | solution.py:283
  35.7 1.1 %collective-permute-done.10.other = f32[3,128,128]{2,1,0:T(8,128)S(1)} collective-permute-done((f32[3,128,128]{2,1,0:T(8,128)S(1)}, f32[3,128,128]{2,1,0:T(8,128)S(1)}, u32[]{:S(2)}, u32[]{:S(2)}) %collective-permute-start.10) | collective-permute-done | bytes 196640 | tf_op jit(solution)/shard_map/ppermute | solution.py:283
  36.8 0.0 copy-done
  36.8 4.7 %shard_map.53 = (f32[128,128]{1,0:T(8,128)}, f32[128,128]{1,0:T(8,128)}, f32[128,128]{1,0:T(8,128)}) custom-call(f32[3,128,128]{2,1,0:T(8,128)S(1)} %get-tuple-element.31.mine, f32[3,128,128]{2,1,0:T(8,128)S(1)} %collective-permute-done.10.other, f32[128,128]{1,0:T(8,128)S(1)} %copy-done, f32[128,128]{1,0:T(8,128)S(1)} %get-tuple-element.32.z_ref), custom_call_target="tpu_custom_call" | custom-call | tf_op jit(solution)/shard_map/pallas_call | solution.py:259
  (9 shorter events, 0.1 us)
Async XLA Ops:
  0.6 0.9 %copy-start.1 = (bf16[64,128]{1,0:T(8,128)(2,1)S(1)}, bf16[64,128]{1,0:T(8,128)(2,1)}, u32[]{:S(2)}) copy-start(bf16[64,128]{1,0:T(8,128)(2,1)} %param.2) | copy-start | bytes 49156
  1.5 6.7 %collective-permute-start = (bf16[1,192,128]{2,1,0:T(8,128)(2,1)S(1)}, bf16[1,192,128]{2,1,0:T(8,128)(2,1)S(1)}, u32[]{:S(2)}, u32[]{:S(2)}) collective-permute-start(bf16[1,192,128]{2,1,0:T(8,128)(2,1)S(1)} %maximum_bitcast_fusion), channel_id=1, source_target_pairs={{0,16},{4,20},{8,24},{12,28},{16,0},{20,4},{24,8},{28,12},{1,17},{... | collective-permute-start | bytes 147464 | tf_op jit(solution)/shard_map/ppermute | solution.py:283
  8.2 4.7 %collective-permute-start.3 = (bf16[2,192,128]{2,1,0:T(8,128)(2,1)S(1)}, bf16[2,192,128]{2,1,0:T(8,128)(2,1)S(1)}, u32[]{:S(2)}, u32[]{:S(2)}) collective-permute-start(bf16[2,192,128]{2,1,0:T(8,128)(2,1)S(1)} %pad_maximum_fusion.1), channel_id=1, source_target_pairs={{0,8},{4,12},{8,0},{12,4},{16,24},{20,28},{24,16},{28,20},{1,9},{5... | collective-permute-start | bytes 294920 | tf_op jit(solution)/shard_map/ppermute | solution.py:283
  12.9 6.9 %collective-permute-start.4 = (bf16[4,192,128]{2,1,0:T(8,128)(2,1)S(1)}, bf16[4,192,128]{2,1,0:T(8,128)(2,1)S(1)}, u32[]{:S(2)}, u32[]{:S(2)}) collective-permute-start(bf16[4,192,128]{2,1,0:T(8,128)(2,1)S(1)} %pad_maximum_fusion.own), channel_id=1, source_target_pairs={{0,4},{4,0},{8,12},{12,8},{16,20},{20,16},{24,28},{28,24},{1,5},{5... | collective-permute-start | bytes 589832 | tf_op jit(solution)/shard_map/ppermute | solution.py:283
  14.7 4.7 %collective-permute-start.1 = (bf16[2,192,128]{2,1,0:T(8,128)(2,1)S(1)}, bf16[2,192,128]{2,1,0:T(8,128)(2,1)S(1)}, u32[]{:S(2)}, u32[]{:S(2)}) collective-permute-start(bf16[2,192,128]{2,1,0:T(8,128)(2,1)S(1)} %pad_maximum_fusion.1), channel_id=1, source_target_pairs={{0,2},{1,3},{2,0},{3,1},{4,6},{5,7},{6,4},{7,5},{8,10},{9,11},{10,... | collective-permute-start | bytes 294920 | tf_op jit(solution)/shard_map/ppermute | solution.py:283
  16.2 10.7 %collective-permute-start.7 = (bf16[4,192,128]{2,1,0:T(8,128)(2,1)S(1)}, bf16[4,192,128]{2,1,0:T(8,128)(2,1)S(1)}, u32[]{:S(2)}, u32[]{:S(2)}) collective-permute-start(bf16[4,192,128]{2,1,0:T(8,128)(2,1)S(1)} %pad_maximum_fusion.own), channel_id=1, source_target_pairs={{0,1},{1,0},{2,3},{3,2},{4,5},{5,4},{6,7},{7,6},{8,9},{9,8},{10,11... | collective-permute-start | bytes 589832 | tf_op jit(solution)/shard_map/ppermute | solution.py:283
  16.2 5.2 %collective-permute-start.8 = (bf16[2,192,128]{2,1,0:T(8,128)(2,1)S(1)}, bf16[2,192,128]{2,1,0:T(8,128)(2,1)S(1)}, u32[]{:S(2)}, u32[]{:S(2)}) collective-permute-start(bf16[2,192,128]{2,1,0:T(8,128)(2,1)S(1)} %collective-permute-done.3), channel_id=1, source_target_pairs={{0,2},{1,3},{2,0},{3,1},{4,6},{5,7},{6,4},{7,5},{8,10},{9,11},{10,... | collective-permute-start | bytes 294920 | tf_op jit(solution)/shard_map/ppermute | solution.py:283
  19.4 4.6 %collective-permute-start.2 = (bf16[2,192,128]{2,1,0:T(8,128)(2,1)S(1)}, bf16[2,192,128]{2,1,0:T(8,128)(2,1)S(1)}, u32[]{:S(2)}, u32[]{:S(2)}) collective-permute-start(bf16[2,192,128]{2,1,0:T(8,128)(2,1)S(1)} %collective-permute-done.1), channel_id=1, source_target_pairs={{0,4},{4,0},{8,12},{12,8},{16,20},{20,16},{24,28},{28,24},{1,5},{5... | collective-permute-start | bytes 294920 | tf_op jit(solution)/shard_map/ppermute | solution.py:283
  21.5 6.1 %collective-permute-start.9 = (bf16[8,192,128]{2,1,0:T(8,128)(2,1)S(1)}, bf16[8,192,128]{2,1,0:T(8,128)(2,1)S(1)}, u32[]{:S(2)}, u32[]{:S(2)}) collective-permute-start(bf16[8,192,128]{2,1,0:T(8,128)(2,1)S(1)} %constant_dynamic-update-slice_fusion.2.own), channel_id=1, source_target_pairs={{0,1},{1,0},{2,3},{3,2},{4,5},{5,4},{6,7},{7,6},{8,9},{9,8},{10,11... | collective-permute-start | bytes 1179656 | tf_op jit(solution)/shard_map/ppermute | solution.py:283
  21.6 5.2 %collective-permute-start.5 = (bf16[2,192,128]{2,1,0:T(8,128)(2,1)S(1)}, bf16[2,192,128]{2,1,0:T(8,128)(2,1)S(1)}, u32[]{:S(2)}, u32[]{:S(2)}) collective-permute-start(bf16[2,192,128]{2,1,0:T(8,128)(2,1)S(1)} %slice.4), channel_id=1, source_target_pairs={{0,2},{1,3},{2,0},{3,1},{4,6},{5,7},{6,4},{7,5},{8,10},{9,11},{10,... | collective-permute-start | bytes 294920 | tf_op jit(solution)/shard_map/ppermute | solution.py:283
  26.8 5.8 %collective-permute-start.6 = (bf16[4,192,128]{2,1,0:T(8,128)(2,1)S(1)}, bf16[4,192,128]{2,1,0:T(8,128)(2,1)S(1)}, u32[]{:S(2)}, u32[]{:S(2)}) collective-permute-start(bf16[4,192,128]{2,1,0:T(8,128)(2,1)S(1)} %constant_dynamic-update-slice_fusion.own), channel_id=1, source_target_pairs={{0,1},{1,0},{2,3},{3,2},{4,5},{5,4},{6,7},{7,6},{8,9},{9,8},{10,11... | collective-permute-start | bytes 589832 | tf_op jit(solution)/shard_map/ppermute | solution.py:283
  32.6 4.2 %copy-start = (f32[128,128]{1,0:T(8,128)S(1)}, f32[128,128]{1,0:T(8,128)}, u32[]{:S(2)}) copy-start(f32[128,128]{1,0:T(8,128)} %targets_ref.1) | copy-start | bytes 196612
  35.2 1.6 %collective-permute-start.10 = (f32[3,128,128]{2,1,0:T(8,128)S(1)}, f32[3,128,128]{2,1,0:T(8,128)S(1)}, u32[]{:S(2)}, u32[]{:S(2)}) collective-permute-start(f32[3,128,128]{2,1,0:T(8,128)S(1)} %get-tuple-element.31.mine), channel_id=1, source_target_pairs={{0,1},{1,0},{2,3},{3,2},{4,5},{5,4},{6,7},{7,6},{8,9},{9,8},{10,11... | collective-permute-start | bytes 589832 | tf_op jit(solution)/shard_map/ppermute | solution.py:283

commit v3 on v2

--- a/solution.py
+++ b/solution.py
@@ -21,7 +21,8 @@
 
 
 def prepare(own, other, left, right, panel, feat_rows):
-    count, _, block = (other if own is None else own).shape
+    block = (other if own is None else own).shape[2]
+    start = other.shape[0] if own is None else own.shape[0]
     ones = jnp.ones((3, block), bf16)
     fill = jnp.zeros((10, block), bf16)
 
@@ -40,10 +41,11 @@
             right[:, here] = jnp.concatenate([feat, ones] + norms + [fill], axis=0)
         panel[:, here] = piece[b, feat_rows:, :]
 
-    for piece, first in ((own, 0), (other, count)):
+    for piece, first in ((own, 0), (other, start)):
         if piece is None:
             continue
-        if count <= 8:
+        count = piece.shape[0]
+        if count <= 12:
             for b in range(count):
                 one(piece, (first + b) * block, b, piece is own)
         else:
@@ -86,8 +88,8 @@
 
 
 def first_kernel(feat_rows, scale):
-    def body(own, other, left, right, panel, y0):
-        prepare(own, other, left, right, panel, feat_rows)
+    def body(own, left, right, panel, y0):
+        prepare(own, None, left, right, panel, feat_rows)
 
         def work(cols, _):
             y0[:, cols] = product((left, panel), right, cols, scale)
@@ -301,23 +303,22 @@
         line = join(features, targets.astype(bf16))[None]
         for axis, bit in hops:
             line = join(line, flip(axis, bit)(line))
-        other_line = partner(line)
         half = line.shape[0] // 2
-        early_y = over_y(line[:half])
-        from_x, late_y = over_x(line), over_y(line[half:])
+        early_y, early_x = over_y(line[:half]), over_x(line[:half])
+        late_x, late_y = over_x(line[half:]), over_y(line[half:])
         far_x = over_x(early_y)
-        near = join(from_x, early_y, late_y)
-        other_near = partner(near)
-        far = join(far_x, over_y(from_x[half:]))
+        near = join(early_x, late_x, early_y)
+        other_near = partner(join(line, near))
+        far = join(far_x, late_y, over_y(late_x))
         other_far = partner(far)
 
         limit = product_vmem if line.shape[0] <= 4 else None
 
-        def stage(count):
+        def stage(row_count, count):
             return [
-                ((2 * count * block, inner_rows), bf16),
+                ((row_count * block, inner_rows), bf16),
                 ((inner_rows, count * block), bf16),
-                ((out_rows, 2 * count * block), bf16),
+                ((out_rows, row_count * block), bf16),
             ]
 
         def sums_of(count):
@@ -328,16 +329,16 @@
 
         n0, n1, n2 = line.shape[0], near.shape[0], far.shape[0]
         left0, right0, panel0, y0 = call(
-            first_kernel(feat_rows, scale), shapes(stage(n0) + [sums_of(n0)]), [], [line, other_line], limit
+            first_kernel(feat_rows, scale), shapes(stage(n0, n0) + [sums_of(n0)]), [], [line], limit
         )
         left1, right1, panel1, y0, y1 = call(
             second_kernel(feat_rows, scale),
-            shapes(stage(n1) + [sums_of(n0), sums_of(n1)]),
+            shapes(stage(n0 + 2 * n1, n1) + [sums_of(n0), sums_of(n1)]),
             [],
             [near, other_near, left0, right0, panel0, y0],
             limit,
         )
-        full_left, right_shape, full_panel = stage(n2)
+        full_left, right_shape, full_panel = stage(2 * n2, n2)
         own_left = ((n2 * block, inner_rows), bf16)
         own_panel = ((out_rows, n2 * block), bf16)
         left2, right2, panel2, y2 = call(

time: 41.7 us -> 38.2 us (0.916)
  waiting for transfers between devices: 14.8 us -> 7.99 us
  starting transfers between devices: 12.1 us -> 15.1 us
    ppermute x11, waiting for transfers between devices: 14.8 us -> 7.99 us  [send(): return lax.ppermute(x, axis, flips(size, bit))]
    ppermute x11, starting transfers between devices: 12.1 us -> 15.1 us  [send(): return lax.ppermute(x, axis, flips(size, bit))]
  transfers between devices with their start and end apart: 11 -> 11, of which waited for: 7 -> 6; matrix products, arithmetic and copies ran while one was open for 0% -> 0% of each run, Pallas kernels for 14% -> 13%
where the time goes in v3:
time: 38.2 us; the launch traced here: 38 us
  starting transfers between devices  15.1 us (40%)
  Pallas kernels  13.1 us (34%)
  waiting for transfers between devices  7.99 us (21%)
  other arithmetic  0.93 us (2%)
  between operations  0.78 us (2%)
    ppermute x11, starting transfers between devices, send(): return lax.ppermute(x, axis, flips(size, bit))  15.1 us
    pallas_call x5, Pallas kernels, call(): pl.pallas_call(kernel, out_shape=out_shape, in_specs=[vmem] * len(operand...  13.1 us
    ppermute x11, waiting for transfers between devices, send(): return lax.ppermute(x, axis, flips(size, bit))  7.99 us
    convert_element_type x1, other arithmetic, step(): line = join(features, targets.astype(bf16))[None]  0.85 us
  transfers between devices with their start and end apart: 11, of which 6 were waited for; matrix products, arithmetic and copies ran while one was open for 0% of the time, Pallas kernels for 13%

profile of v3, /device:TPU:0, one launch (start us, length us, event | category | flops | bytes accessed | tf_op | source)
XLA Modules:
  0.0 38.0 jit_solution(11239530690101334019)
XLA Ops:
  0.6 0.0 copy-start.1
  0.6 0.9 %convert_element_type.3 = bf16[128,128]{1,0:T(8,128)(2,1)S(1)} convert(f32[128,128]{1,0:T(8,128)} %targets_ref.1) | non-fusion elementwise | flops 16384 | bytes 98304 | tf_op jit(solution)/shard_map/convert_element_type | solution.py:303
  1.5 0.0 copy-done.1
  1.5 4.1 %collective-permute-start = (bf16[1,192,128]{2,1,0:T(8,128)(2,1)S(1)}, bf16[1,192,128]{2,1,0:T(8,128)(2,1)S(1)}, u32[]{:S(2)}, u32[]{:S(2)}) collective-permute-start(bf16[1,192,128]{2,1,0:T(8,128)(2,1)S(1)} %maximum_bitcast_fusion), channel_id=1, source_target_pairs={{0,16},{4,20},{8,24},{12,28},{16,0},{20,4},{24,8},{28,12},{1,17},{... | collective-permute-start | bytes 147464 | tf_op jit(solution)/shard_map/ppermute | solution.py:285
  5.6 2.6 %collective-permute-done = bf16[1,192,128]{2,1,0:T(8,128)(2,1)S(1)} collective-permute-done((bf16[1,192,128]{2,1,0:T(8,128)(2,1)S(1)}, bf16[1,192,128]{2,1,0:T(8,128)(2,1)S(1)}, u32[]{:S(2)}, u32[]{:S(2)}) %collective-permute-start) | collective-permute-done | bytes 49184 | tf_op jit(solution)/shard_map/ppermute | solution.py:285
  8.2 1.4 %collective-permute-start.3 = (bf16[2,192,128]{2,1,0:T(8,128)(2,1)S(1)}, bf16[2,192,128]{2,1,0:T(8,128)(2,1)S(1)}, u32[]{:S(2)}, u32[]{:S(2)}) collective-permute-start(bf16[2,192,128]{2,1,0:T(8,128)(2,1)S(1)} %pad_maximum_fusion.2), channel_id=1, source_target_pairs={{0,8},{4,12},{8,0},{12,4},{16,24},{20,28},{24,16},{28,20},{1,9},{5... | collective-permute-start | bytes 294920 | tf_op jit(solution)/shard_map/ppermute | solution.py:285
  9.7 1.5 %collective-permute-start.8 = (bf16[2,192,128]{2,1,0:T(8,128)(2,1)S(1)}, bf16[2,192,128]{2,1,0:T(8,128)(2,1)S(1)}, u32[]{:S(2)}, u32[]{:S(2)}) collective-permute-start(bf16[2,192,128]{2,1,0:T(8,128)(2,1)S(1)} %pad_maximum_fusion.2), channel_id=1, source_target_pairs={{0,4},{4,0},{8,12},{12,8},{16,20},{20,16},{24,28},{28,24},{1,5},{5... | collective-permute-start | bytes 294920 | tf_op jit(solution)/shard_map/ppermute | solution.py:285
  11.2 1.5 %collective-permute-start.1 = (bf16[2,192,128]{2,1,0:T(8,128)(2,1)S(1)}, bf16[2,192,128]{2,1,0:T(8,128)(2,1)S(1)}, u32[]{:S(2)}, u32[]{:S(2)}) collective-permute-start(bf16[2,192,128]{2,1,0:T(8,128)(2,1)S(1)} %pad_maximum_fusion.2), channel_id=1, source_target_pairs={{0,2},{1,3},{2,0},{3,1},{4,6},{5,7},{6,4},{7,5},{8,10},{9,11},{10,... | collective-permute-start | bytes 294920 | tf_op jit(solution)/shard_map/ppermute | solution.py:285
  12.7 0.2 collective-permute-done.3
  12.9 1.7 %collective-permute-start.5 = (bf16[2,192,128]{2,1,0:T(8,128)(2,1)S(1)}, bf16[2,192,128]{2,1,0:T(8,128)(2,1)S(1)}, u32[]{:S(2)}, u32[]{:S(2)}) collective-permute-start(bf16[2,192,128]{2,1,0:T(8,128)(2,1)S(1)} %collective-permute-done.3), channel_id=1, source_target_pairs={{0,4},{4,0},{8,12},{12,8},{16,20},{20,16},{24,28},{28,24},{1,5},{5... | collective-permute-start | bytes 294920 | tf_op jit(solution)/shard_map/ppermute | solution.py:285
  14.6 1.5 %collective-permute-start.4 = (bf16[2,192,128]{2,1,0:T(8,128)(2,1)S(1)}, bf16[2,192,128]{2,1,0:T(8,128)(2,1)S(1)}, u32[]{:S(2)}, u32[]{:S(2)}) collective-permute-start(bf16[2,192,128]{2,1,0:T(8,128)(2,1)S(1)} %collective-permute-done.3), channel_id=1, source_target_pairs={{0,2},{1,3},{2,0},{3,1},{4,6},{5,7},{6,4},{7,5},{8,10},{9,11},{10,... | collective-permute-start | bytes 294920 | tf_op jit(solution)/shard_map/ppermute | solution.py:285
  16.1 0.0 collective-permute-done.1
  16.2 0.9 %collective-permute-start.2 = (bf16[2,192,128]{2,1,0:T(8,128)(2,1)S(1)}, bf16[2,192,128]{2,1,0:T(8,128)(2,1)S(1)}, u32[]{:S(2)}, u32[]{:S(2)}) collective-permute-start(bf16[2,192,128]{2,1,0:T(8,128)(2,1)S(1)} %collective-permute-done.1), channel_id=1, source_target_pairs={{0,4},{4,0},{8,12},{12,8},{16,20},{20,16},{24,28},{28,24},{1,5},{5... | collective-permute-start | bytes 294920 | tf_op jit(solution)/shard_map/ppermute | solution.py:285
  17.1 0.0 collective-permute-done.8
  17.2 0.6 %collective-permute-done.5 = bf16[2,192,128]{2,1,0:T(8,128)(2,1)S(1)} collective-permute-done((bf16[2,192,128]{2,1,0:T(8,128)(2,1)S(1)}, bf16[2,192,128]{2,1,0:T(8,128)(2,1)S(1)}, u32[]{:S(2)}, u32[]{:S(2)}) %collective-permute-start.5) | collective-permute-done | bytes 98336 | tf_op jit(solution)/shard_map/ppermute | solution.py:285
  17.8 0.1 collective-permute-start.9
  17.9 1.6 %collective-permute-start.6 = (bf16[2,192,128]{2,1,0:T(8,128)(2,1)S(1)}, bf16[2,192,128]{2,1,0:T(8,128)(2,1)S(1)}, u32[]{:S(2)}, u32[]{:S(2)}) collective-permute-start(bf16[2,192,128]{2,1,0:T(8,128)(2,1)S(1)} %collective-permute-done.5), channel_id=1, source_target_pairs={{0,2},{1,3},{2,0},{3,1},{4,6},{5,7},{6,4},{7,5},{8,10},{9,11},{10,... | collective-permute-start | bytes 294920 | tf_op jit(solution)/shard_map/ppermute | solution.py:285
  19.5 1.3 %collective-permute-done.2 = bf16[2,192,128]{2,1,0:T(8,128)(2,1)S(1)} collective-permute-done((bf16[2,192,128]{2,1,0:T(8,128)(2,1)S(1)}, bf16[2,192,128]{2,1,0:T(8,128)(2,1)S(1)}, u32[]{:S(2)}, u32[]{:S(2)}) %collective-permute-start.2) | collective-permute-done | bytes 98336 | tf_op jit(solution)/shard_map/ppermute | solution.py:285
  20.8 0.0 collective-permute-done.4
  20.8 2.2 %collective-permute-done.6 = bf16[2,192,128]{2,1,0:T(8,128)(2,1)S(1)} collective-permute-done((bf16[2,192,128]{2,1,0:T(8,128)(2,1)S(1)}, bf16[2,192,128]{2,1,0:T(8,128)(2,1)S(1)}, u32[]{:S(2)}, u32[]{:S(2)}) %collective-permute-start.6) | collective-permute-done | bytes 98336 | tf_op jit(solution)/shard_map/ppermute | solution.py:285
  23.1 0.1 collective-permute-start.7
  23.2 0.5 %shard_map.49 = (bf16[512,80]{1,0:T(8,128)(2,1)S(1)}, bf16[80,512]{1,0:T(8,128)(2,1)S(1)}, bf16[128,512]{1,0:T(8,128)(2,1)S(1)}, f32[128,512]{1,0:T(8,128)S(1)}) custom-call(bf16[4,192,128]{2,1,0:T(8,128)(2,1)S(1)} %pad_maximum_fusion.1.own), custom_call_target="tpu_custom_call" | custom-call | tf_op jit(solution)/shard_map/pallas_call | solution.py:261
  23.8 0.0 collective-permute-done.9.other
  23.8 2.6 %shard_map.50 = (bf16[2048,80]{1,0:T(8,128)(2,1)S(1)}, bf16[80,768]{1,0:T(8,128)(2,1)S(1)}, bf16[128,2048]{1,0:T(8,128)(2,1)S(1)}, f32[128,512]{1,0:T(8,128)S(1)}, f32[128,768]{1,0:T(8,128)S(1)}) custom-call(bf16[6,192,128]{2,1,0:T(8,128)(2,1)S(1)} %pad_maximum_fusion.own, bf16[10,192,128]{2,1,0:T(8,128)(2,1)S(1)} %collective-permute-done.9.other, ...), custom_call_target="tpu_custom_call" | custom-call | tf_op jit(solution)/shard_map/pallas_call | solution.py:261
  26.4 1.8 %shard_map.51 = (bf16[768,80]{1,0:T(8,128)(2,1)S(1)}, bf16[80,768]{1,0:T(8,128)(2,1)S(1)}, bf16[128,768]{1,0:T(8,128)(2,1)S(1)}, f32[128,768]{1,0:T(8,128)S(1)}) custom-call(bf16[6,192,128]{2,1,0:T(8,128)(2,1)S(1)} %constant_dynamic-update-slice_fusion.own, bf16[512,80]{1,0:T(8,128)(2,1)S(1)} %get-tuple-element.18.left0, ...), custom_call_target="tpu_custom_call" | custom-call | tf_op jit(solution)/shard_map/pallas_call | solution.py:261
  28.2 0.0 collective-permute-done.7.other
  28.2 0.0 copy-start
  28.2 3.4 %shard_map.52 = (f32[128,128]{1,0:T(8,128)S(1)}, f32[3,128,128]{2,1,0:T(8,128)S(1)}) custom-call(bf16[6,192,128]{2,1,0:T(8,128)(2,1)S(1)} %collective-permute-done.7.other, bf16[768,80]{1,0:T(8,128)(2,1)S(1)} %get-tuple-element.24.refs_0_, bf16[80,768]{1,0:T(8,128)(2,1)S(1)} %get-tuple-element.25.refs_1_, bf16[128,768]{1,0:T(8,128)(2,1)S(1)} %get-tuple-element.26.refs_2_, ...), custom_call_target="tpu_custom_call" | custom-call | tf_op jit(solution)/shard_map/pallas_call | solution.py:261
  31.7 0.6 %collective-permute-start.10 = (f32[3,128,128]{2,1,0:T(8,128)S(1)}, f32[3,128,128]{2,1,0:T(8,128)S(1)}, u32[]{:S(2)}, u32[]{:S(2)}) collective-permute-start(f32[3,128,128]{2,1,0:T(8,128)S(1)} %get-tuple-element.31.mine), channel_id=1, source_target_pairs={{0,1},{1,0},{2,3},{3,2},{4,5},{5,4},{6,7},{7,6},{8,9},{9,8},{10,11... | collective-permute-start | bytes 589832 | tf_op jit(solution)/shard_map/ppermute | solution.py:285
  32.2 1.1 %collective-permute-done.10.other = f32[3,128,128]{2,1,0:T(8,128)S(1)} collective-permute-done((f32[3,128,128]{2,1,0:T(8,128)S(1)}, f32[3,128,128]{2,1,0:T(8,128)S(1)}, u32[]{:S(2)}, u32[]{:S(2)}) %collective-permute-start.10) | collective-permute-done | bytes 196640 | tf_op jit(solution)/shard_map/ppermute | solution.py:285
  33.3 0.0 copy-done
  33.3 4.7 %shard_map.53 = (f32[128,128]{1,0:T(8,128)}, f32[128,128]{1,0:T(8,128)}, f32[128,128]{1,0:T(8,128)}) custom-call(f32[3,128,128]{2,1,0:T(8,128)S(1)} %get-tuple-element.31.mine, f32[3,128,128]{2,1,0:T(8,128)S(1)} %collective-permute-done.10.other, f32[128,128]{1,0:T(8,128)S(1)} %copy-done, f32[128,128]{1,0:T(8,128)S(1)} %get-tuple-element.32.z_ref), custom_call_target="tpu_custom_call" | custom-call | tf_op jit(solution)/shard_map/pallas_call | solution.py:261
  (13 shorter events, 0.2 us)
Async XLA Ops:
  0.6 0.9 %copy-start.1 = (bf16[64,128]{1,0:T(8,128)(2,1)S(1)}, bf16[64,128]{1,0:T(8,128)(2,1)}, u32[]{:S(2)}) copy-start(bf16[64,128]{1,0:T(8,128)(2,1)} %param.2) | copy-start | bytes 49156
  1.5 6.7 %collective-permute-start = (bf16[1,192,128]{2,1,0:T(8,128)(2,1)S(1)}, bf16[1,192,128]{2,1,0:T(8,128)(2,1)S(1)}, u32[]{:S(2)}, u32[]{:S(2)}) collective-permute-start(bf16[1,192,128]{2,1,0:T(8,128)(2,1)S(1)} %maximum_bitcast_fusion), channel_id=1, source_target_pairs={{0,16},{4,20},{8,24},{12,28},{16,0},{20,4},{24,8},{28,12},{1,17},{... | collective-permute-start | bytes 147464 | tf_op jit(solution)/shard_map/ppermute | solution.py:285
  8.2 4.7 %collective-permute-start.3 = (bf16[2,192,128]{2,1,0:T(8,128)(2,1)S(1)}, bf16[2,192,128]{2,1,0:T(8,128)(2,1)S(1)}, u32[]{:S(2)}, u32[]{:S(2)}) collective-permute-start(bf16[2,192,128]{2,1,0:T(8,128)(2,1)S(1)} %pad_maximum_fusion.2), channel_id=1, source_target_pairs={{0,8},{4,12},{8,0},{12,4},{16,24},{20,28},{24,16},{28,20},{1,9},{5... | collective-permute-start | bytes 294920 | tf_op jit(solution)/shard_map/ppermute | solution.py:285
  9.7 7.4 %collective-permute-start.8 = (bf16[2,192,128]{2,1,0:T(8,128)(2,1)S(1)}, bf16[2,192,128]{2,1,0:T(8,128)(2,1)S(1)}, u32[]{:S(2)}, u32[]{:S(2)}) collective-permute-start(bf16[2,192,128]{2,1,0:T(8,128)(2,1)S(1)} %pad_maximum_fusion.2), channel_id=1, source_target_pairs={{0,4},{4,0},{8,12},{12,8},{16,20},{20,16},{24,28},{28,24},{1,5},{5... | collective-permute-start | bytes 294920 | tf_op jit(solution)/shard_map/ppermute | solution.py:285
  11.2 5.0 %collective-permute-start.1 = (bf16[2,192,128]{2,1,0:T(8,128)(2,1)S(1)}, bf16[2,192,128]{2,1,0:T(8,128)(2,1)S(1)}, u32[]{:S(2)}, u32[]{:S(2)}) collective-permute-start(bf16[2,192,128]{2,1,0:T(8,128)(2,1)S(1)} %pad_maximum_fusion.2), channel_id=1, source_target_pairs={{0,2},{1,3},{2,0},{3,1},{4,6},{5,7},{6,4},{7,5},{8,10},{9,11},{10,... | collective-permute-start | bytes 294920 | tf_op jit(solution)/shard_map/ppermute | solution.py:285
  12.9 4.8 %collective-permute-start.5 = (bf16[2,192,128]{2,1,0:T(8,128)(2,1)S(1)}, bf16[2,192,128]{2,1,0:T(8,128)(2,1)S(1)}, u32[]{:S(2)}, u32[]{:S(2)}) collective-permute-start(bf16[2,192,128]{2,1,0:T(8,128)(2,1)S(1)} %collective-permute-done.3), channel_id=1, source_target_pairs={{0,4},{4,0},{8,12},{12,8},{16,20},{20,16},{24,28},{28,24},{1,5},{5... | collective-permute-start | bytes 294920 | tf_op jit(solution)/shard_map/ppermute | solution.py:285
  14.6 6.2 %collective-permute-start.4 = (bf16[2,192,128]{2,1,0:T(8,128)(2,1)S(1)}, bf16[2,192,128]{2,1,0:T(8,128)(2,1)S(1)}, u32[]{:S(2)}, u32[]{:S(2)}) collective-permute-start(bf16[2,192,128]{2,1,0:T(8,128)(2,1)S(1)} %collective-permute-done.3), channel_id=1, source_target_pairs={{0,2},{1,3},{2,0},{3,1},{4,6},{5,7},{6,4},{7,5},{8,10},{9,11},{10,... | collective-permute-start | bytes 294920 | tf_op jit(solution)/shard_map/ppermute | solution.py:285
  16.2 4.6 %collective-permute-start.2 = (bf16[2,192,128]{2,1,0:T(8,128)(2,1)S(1)}, bf16[2,192,128]{2,1,0:T(8,128)(2,1)S(1)}, u32[]{:S(2)}, u32[]{:S(2)}) collective-permute-start(bf16[2,192,128]{2,1,0:T(8,128)(2,1)S(1)} %collective-permute-done.1), channel_id=1, source_target_pairs={{0,4},{4,0},{8,12},{12,8},{16,20},{20,16},{24,28},{28,24},{1,5},{5... | collective-permute-start | bytes 294920 | tf_op jit(solution)/shard_map/ppermute | solution.py:285
  17.8 6.0 %collective-permute-start.9 = (bf16[10,192,128]{2,1,0:T(8,128)(2,1)S(1)}, bf16[10,192,128]{2,1,0:T(8,128)(2,1)S(1)}, u32[]{:S(2)}, u32[]{:S(2)}) collective-permute-start(bf16[10,192,128]{2,1,0:T(8,128)(2,1)S(1)} %constant_dynamic-update-slice_fusion.3), channel_id=1, source_target_pairs={{0,1},{1,0},{2,3},{3,2},{4,5},{5,4},{6,7},{7,6},{8,9},{9,8},{10,11... | collective-permute-start | bytes 1474568 | tf_op jit(solution)/shard_map/ppermute | solution.py:285
  17.9 5.2 %collective-permute-start.6 = (bf16[2,192,128]{2,1,0:T(8,128)(2,1)S(1)}, bf16[2,192,128]{2,1,0:T(8,128)(2,1)S(1)}, u32[]{:S(2)}, u32[]{:S(2)}) collective-permute-start(bf16[2,192,128]{2,1,0:T(8,128)(2,1)S(1)} %collective-permute-done.5), channel_id=1, source_target_pairs={{0,2},{1,3},{2,0},{3,1},{4,6},{5,7},{6,4},{7,5},{8,10},{9,11},{10,... | collective-permute-start | bytes 294920 | tf_op jit(solution)/shard_map/ppermute | solution.py:285
  23.1 5.2 %collective-permute-start.7 = (bf16[6,192,128]{2,1,0:T(8,128)(2,1)S(1)}, bf16[6,192,128]{2,1,0:T(8,128)(2,1)S(1)}, u32[]{:S(2)}, u32[]{:S(2)}) collective-permute-start(bf16[6,192,128]{2,1,0:T(8,128)(2,1)S(1)} %constant_dynamic-update-slice_fusion.own), channel_id=1, source_target_pairs={{0,1},{1,0},{2,3},{3,2},{4,5},{5,4},{6,7},{7,6},{8,9},{9,8},{10,11... | collective-permute-start | bytes 884744 | tf_op jit(solution)/shard_map/ppermute | solution.py:285
  28.2 5.1 %copy-start = (f32[128,128]{1,0:T(8,128)S(1)}, f32[128,128]{1,0:T(8,128)}, u32[]{:S(2)}) copy-start(f32[128,128]{1,0:T(8,128)} %targets_ref.1) | copy-start | bytes 196612
  31.7 1.6 %collective-permute-start.10 = (f32[3,128,128]{2,1,0:T(8,128)S(1)}, f32[3,128,128]{2,1,0:T(8,128)S(1)}, u32[]{:S(2)}, u32[]{:S(2)}) collective-permute-start(f32[3,128,128]{2,1,0:T(8,128)S(1)} %get-tuple-element.31.mine), channel_id=1, source_target_pairs={{0,1},{1,0},{2,3},{3,2},{4,5},{5,4},{6,7},{7,6},{8,9},{9,8},{10,11... | collective-permute-start | bytes 589832 | tf_op jit(solution)/shard_map/ppermute | solution.py:285
